TPU v7x, 1024 devices: a whole 4x8x16 slice. The times are simulated.
1024 devices in a mesh: ctx: 16 (over x_hi, y), dp: 64 (over z, x_lo, core).
Axes of the slice: x: 4 (x_hi: 2, x_lo: 2; x = x_hi * 2 + x_lo), y: 8, z: 16, core: 2. Of those that a mesh axis runs over, the one named last changes fastest.
Arguments:
- queries: bfloat16 [64, 16384, 128], P('dp', 'ctx'), may hold values from -24 to 24
- keys: bfloat16 [64, 16384, 128], P('dp', 'ctx'), may hold values from -24 to 24
- values: bfloat16 [64, 16384, 128], P('dp', 'ctx'), may hold values from -6 to 6
- grad_out: bfloat16 [64, 16384, 128], P('dp', 'ctx'), may hold values from -6 to 6
- gain: float32 [1024], P('dp'), may hold values from 0.1 to 1.9
- doc_start: int32 [8, 16384], replicated, may hold values from 0 to 16383, as said below
- win_start: int32 [8, 16384], replicated, may hold values from 0 to 16256, as said below
Outputs:
- grad_queries: bfloat16 [64, 16384, 128], P('dp', 'ctx')
- grad_keys: bfloat16 [64, 16384, 128], P('dp', 'ctx')
- grad_values: bfloat16 [64, 16384, 128], P('dp', 'ctx')
- grad_gain: float32 [1024], P('dp')
Inputs may be any that keep to these rules, and one draw needn't show every extreme that they name: Documents are contiguous runs of positions: doc_start of a row is at most its position, equals its own position at a document's first row, and is the same for all rows of a document. win_start is a multiple of 128, at most the start of the row's block of 128 positions and at least (7) * 128 positions before that start.
All inputs are finite; a program needn't handle non-finite values.
Results may differ from a plain program's by a relative error of at most 0.012.
The roundings to bfloat16 on the way count: a program that leaves them out, or rounds other values in their place, can miss the bound.
Values may be sent and summed in bfloat16 or wider, within the bound.
A program may use at most 64 MiB of HBM per device.

v0:
```python
import math

import jax
import jax.numpy as jnp
from jax import lax
from jax.sharding import PartitionSpec as P

HEADS = 8
BLK = 128
WBLK = 8


def from_behind(value, axis, by):
    length = lax.axis_size(axis)
    pairs = [(i, i + by) for i in range(length) if 0 <= i + by < length]
    return lax.ppermute(value, axis, pairs)


def block_scores(left_rows, right_rows):
    return jnp.einsum("bnqd,bnkd->bnqk", left_rows, right_rows, preferred_element_type=jnp.float32)


def block_mix(weights, right_rows):
    return jnp.einsum("bnqk,bnkd->bnqd", weights, right_rows, preferred_element_type=jnp.float32)


def block_back(weights, left_rows):
    return jnp.einsum("bnqk,bnqd->bnkd", weights, left_rows, preferred_element_type=jnp.float32)


def spread(parts, pair_count, group_rows, head_width):
    summed = jnp.zeros((pair_count, (WBLK - 1) * BLK + group_rows, head_width), jnp.float32)
    for offset in range(WBLK):
        slab_rows = parts[offset].reshape(pair_count, group_rows, head_width)
        summed = summed + jnp.pad(
            slab_rows, ((0, 0), (offset * BLK, (WBLK - 1 - offset) * BLK), (0, 0))
        )
    return summed


def band_mask(first_row, lower_bound, nblock):
    query_pos = (first_row + jnp.arange(nblock * BLK, dtype=jnp.int32)).reshape(nblock, BLK)
    key_pos = (
        first_row
        - (WBLK - 1) * BLK
        + (jnp.arange(nblock, dtype=jnp.int32) * BLK)[:, None]
        + jnp.arange(WBLK * BLK, dtype=jnp.int32)[None, :]
    )
    return (key_pos[:, None, :] >= lower_bound.reshape(nblock, BLK)[:, :, None]) & (
        key_pos[:, None, :] <= query_pos[:, :, None]
    )


def band_terms(query_blocks, grad_blocks, key_window, value_window, visible, score_scale):
    pair_count, nblock, blk_rows, head_width = query_blocks.shape
    group_rows = nblock * blk_rows
    key_slabs = [
        key_window[:, offset * blk_rows : offset * blk_rows + group_rows].reshape(
            pair_count, nblock, blk_rows, head_width
        )
        for offset in range(WBLK)
    ]
    value_slabs = [
        value_window[:, offset * blk_rows : offset * blk_rows + group_rows].reshape(
            pair_count, nblock, blk_rows, head_width
        )
        for offset in range(WBLK)
    ]
    slab_shape = (pair_count, nblock, blk_rows, head_width)
    scores = (
        jnp.concatenate(
            [block_scores(query_blocks, key_slabs[offset]) for offset in range(WBLK)], axis=-1
        )
        * score_scale
    )
    scores = jnp.where(visible[None], scores, -jnp.inf)
    weights = jnp.exp(scores - jnp.max(scores, axis=-1, keepdims=True))
    attn_probs = (weights / jnp.sum(weights, axis=-1, keepdims=True)).astype(jnp.bfloat16)
    prob_grad = jnp.concatenate(
        [block_scores(grad_blocks, value_slabs[offset]) for offset in range(WBLK)], axis=-1
    )
    row_delta = jnp.sum(attn_probs.astype(jnp.float32) * prob_grad, axis=-1, keepdims=True)
    score_grad = (attn_probs.astype(jnp.float32) * (prob_grad - row_delta)).astype(jnp.bfloat16)
    mixed = jnp.zeros(slab_shape, jnp.float32)
    key_parts = []
    value_parts = []
    for offset in range(WBLK):
        score_slab = score_grad[..., offset * blk_rows : (offset + 1) * blk_rows]
        prob_slab = attn_probs[..., offset * blk_rows : (offset + 1) * blk_rows]
        mixed = mixed + block_mix(score_slab, key_slabs[offset])
        key_parts.append(block_back(score_slab, query_blocks) * score_scale)
        value_parts.append(block_back(prob_slab, grad_blocks))
    return (
        mixed * score_scale,
        spread(key_parts, pair_count, group_rows, head_width),
        spread(value_parts, pair_count, group_rows, head_width),
    )


def on_device(queries, keys, values, grad_out, gain, doc_start, win_start):
    pair_count, tok_rows, head_width = queries.shape
    nblock = tok_rows // BLK
    group_blocks = math.gcd(nblock, max(1, 512 // BLK))
    group_rows = group_blocks * BLK
    prev_rows = (WBLK - 1) * BLK
    span_rows = prev_rows + group_rows
    score_scale = 1.0 / math.sqrt(head_width)
    first_row = lax.axis_index("ctx") * tok_rows
    first_pair = lax.axis_index("dp") * pair_count
    head_first = first_pair % HEADS
    seq_index = first_pair // HEADS
    full_gain = lax.all_gather(gain, "dp", axis=0, tiled=True)
    gain_rows = lax.dynamic_slice_in_dim(
        full_gain.reshape(HEADS, head_width), head_first, pair_count, 0
    )
    scaled = (queries.astype(jnp.float32) * gain_rows[:, None, :]).astype(jnp.bfloat16)
    earlier = from_behind(
        (keys[:, tok_rows - prev_rows :], values[:, tok_rows - prev_rows :]), "ctx", 1
    )
    key_ext = jnp.concatenate([earlier[0], keys], axis=1)
    value_ext = jnp.concatenate([earlier[1], values], axis=1)
    seq_docs = lax.dynamic_index_in_dim(doc_start, seq_index, 0, keepdims=False)
    seq_wins = lax.dynamic_index_in_dim(win_start, seq_index, 0, keepdims=False)
    lower_full = jnp.maximum(seq_docs, seq_wins)
    lower_bound = lax.dynamic_slice_in_dim(lower_full, first_row, tok_rows, 0)
    visible = band_mask(first_row, lower_bound, nblock)
    query_blocks = scaled.reshape(pair_count, nblock, BLK, head_width)
    grad_blocks = grad_out.reshape(pair_count, nblock, BLK, head_width)

    def group_step(group_index, state_tuple):
        grad_scaled, key_grad, value_grad = state_tuple
        block_first = group_index * group_blocks
        row_first = block_first * BLK
        grad_piece, key_piece, value_piece = band_terms(
            lax.dynamic_slice_in_dim(query_blocks, block_first, group_blocks, 1),
            lax.dynamic_slice_in_dim(grad_blocks, block_first, group_blocks, 1),
            lax.dynamic_slice_in_dim(key_ext, row_first, span_rows, 1),
            lax.dynamic_slice_in_dim(value_ext, row_first, span_rows, 1),
            lax.dynamic_slice_in_dim(visible, block_first, group_blocks, 0),
            score_scale,
        )
        grad_scaled = lax.dynamic_update_slice_in_dim(grad_scaled, grad_piece, block_first, 1)
        key_grad = lax.dynamic_update_slice_in_dim(
            key_grad,
            lax.dynamic_slice_in_dim(key_grad, row_first, span_rows, 1) + key_piece,
            row_first,
            1,
        )
        value_grad = lax.dynamic_update_slice_in_dim(
            value_grad,
            lax.dynamic_slice_in_dim(value_grad, row_first, span_rows, 1) + value_piece,
            row_first,
            1,
        )
        return (grad_scaled, key_grad, value_grad)

    initial = (
        jnp.zeros((pair_count, nblock, BLK, head_width), jnp.float32),
        jnp.zeros((pair_count, prev_rows + tok_rows, head_width), jnp.float32),
        jnp.zeros((pair_count, prev_rows + tok_rows, head_width), jnp.float32),
    )
    grad_scaled, key_ext_grad, value_ext_grad = lax.fori_loop(
        0, nblock // group_blocks, group_step, initial
    )
    grad_scaled = grad_scaled.reshape(pair_count, tok_rows, head_width)
    key_own = key_ext_grad[:, prev_rows:]
    value_own = value_ext_grad[:, prev_rows:]
    returned = from_behind(
        (
            key_ext_grad[:, :prev_rows].astype(jnp.bfloat16),
            value_ext_grad[:, :prev_rows].astype(jnp.bfloat16),
        ),
        "ctx",
        -1,
    )
    key_own = key_own.at[:, tok_rows - prev_rows :].add(returned[0].astype(jnp.float32))
    value_own = value_own.at[:, tok_rows - prev_rows :].add(returned[1].astype(jnp.float32))
    grad_queries = (grad_scaled * gain_rows[:, None, :]).astype(jnp.bfloat16)
    head_terms = jnp.sum(grad_scaled * queries.astype(jnp.float32), axis=1)
    gain_table = lax.dynamic_update_slice_in_dim(
        jnp.zeros((HEADS, head_width), jnp.float32), head_terms, head_first, 0
    ).reshape(HEADS * head_width)
    everything = lax.psum(gain_table, ("ctx", "dp"))
    share_len = everything.shape[0] // lax.axis_size("dp")
    grad_gain = lax.dynamic_slice_in_dim(everything, lax.axis_index("dp") * share_len, share_len, 0)
    return (grad_queries, key_own.astype(jnp.bfloat16), value_own.astype(jnp.bfloat16), grad_gain)


def solution(mesh):
    placed = (
        P("dp", "ctx", None),
        P("dp", "ctx", None),
        P("dp", "ctx", None),
        P("dp", "ctx", None),
        P("dp"),
        P(),
        P(),
    )
    return jax.shard_map(
        on_device,
        mesh=mesh,
        in_specs=placed,
        out_specs=(P("dp", "ctx", None), P("dp", "ctx", None), P("dp", "ctx", None), P("dp")),
        check_vma=False,
    )
```

profile of v0, /device:TPU:1, one launch (start us, length us, event | category | flops | bytes accessed | tf_op | source)
XLA Modules:
  0.0 305.1 jit_solution(5823917216532653487)
XLA Ops:
  0.7 1.0 slice.390
  1.7 4.0 %collective-permute-start = (bf16[1,896,128]{2,1,0:T(8,128)(2,1)S(1)}, bf16[1,896,128]{2,1,0:T(8,128)(2,1)S(1)}, u32[]{:S(2)}, u32[]{:S(2)}) collective-permute-start(bf16[1,896,128]{2,1,0:T(8,128)(2,1)S(1)} %slice.390), channel_id=1, source_target_pairs={{0,64},{64,128},{128,192},{192,256},{256,320},{320,384},{384,448},... | collective-permute-start | bytes 688136 | tf_op jit(solution)/shard_map/ppermute | solution.py:16
  5.7 1.0 slice.391
  6.7 3.2 %collective-permute-start.1 = (bf16[1,896,128]{2,1,0:T(8,128)(2,1)S(1)}, bf16[1,896,128]{2,1,0:T(8,128)(2,1)S(1)}, u32[]{:S(2)}, u32[]{:S(2)}) collective-permute-start(bf16[1,896,128]{2,1,0:T(8,128)(2,1)S(1)} %slice.391), channel_id=1, source_target_pairs={{0,64},{64,128},{128,192},{192,256},{256,320},{320,384},{384,448},... | collective-permute-start | bytes 688136 | tf_op jit(solution)/shard_map/ppermute | solution.py:16
  10.1 1.3 dynamic-slice.17
  12.0 0.9 dynamic-update-slice.6
  12.9 118.8 %all-reduce.17 = f32[8,128]{1,0:T(8,128)S(1)} all-reduce(f32[8,128]{1,0:T(8,128)S(1)} %bitcast.481), channel_id=1, replica_groups=mesh['ctx'=16,'dp'=64] {'dp'}, use_global_device_ids=true, to_apply=%add.16 | all-reduce | flops 1024 | bytes 8192
  131.6 0.9 dynamic-slice_maximum_fusion
  132.5 3.5 %compare_and_fusion = pred[8,128,1024]{1,2,0:T(8,128)(4,1)} fusion(s32[8,128]{1,0:T(8,128)S(1)} %add_add_fusion, s32[8,128]{1,0:T(8,128)S(1)} %bitcast.479, s32[8,1024]{1,0:T(8,128)S(1)} %iota_add_fusion), kind=kLoop, calls=%fused_computation.131 | loop fusion | flops 3145728 | bytes 1089536 | tf_op jit(solution)/shard_map/and | solution.py:49
  136.2 0.8 broadcast_in_dim.30
  137.1 1.0 broadcast.201.clone
  138.2 34.1 %while.21 = (s32[]{:T(128)}, f32[1,8,128,128]{3,2,1,0:T(8,128)}, f32[1,1920,128]{2,1,0:T(8,128)S(1)}, f32[1,1920,128]{2,1,0:T(8,128)}, pred[8,128,1024]{1,2,0:T(...) while((s32[]{:T(128)}, f32[1,8,128,128]{3,2,1,0:T(8,128)}, ...), condition=%wide.region_4.5_spmd, body=%wide.region_0.4_spmd.sunk | while | flops 680792576 | bytes 79168672 | solution.py:162
  138.7 0.2 convolution_dynamic-update-slice_fusion.33
  138.9 0.2 convolution_dynamic-update-slice_fusion.34
  139.1 0.2 convolution_dynamic-update-slice_fusion.35
  139.5 0.2 convolution_dynamic-update-slice_fusion.37
  139.8 0.2 convolution_dynamic-update-slice_fusion.38
  140.0 0.2 convolution_dynamic-update-slice_fusion.39
  140.2 0.2 convolution_dynamic-update-slice_fusion.40
  140.4 0.2 convolution_dynamic-update-slice_fusion.41
  141.1 0.2 convolution_dynamic-update-slice_fusion.44
  141.3 0.2 convolution_dynamic-update-slice_fusion.45
  142.0 1.3 copy-done.27
  143.3 2.5 divide_convert_fusion.2
  145.8 2.9 fusion.213
  148.8 0.2 fusion.214
  149.0 0.2 convolution_add_fusion.13
  149.3 0.2 convolution_add_fusion.14
  149.6 0.2 convolution_add_fusion.15
  149.8 0.2 convolution_add_fusion.16
  150.1 0.2 convolution_add_fusion.17
  150.3 0.2 convolution_add_fusion.18
  150.6 0.2 fusion.215
  153.8 0.4 add_dynamic-update-slice_fusion.5
  154.3 1.0 copy-done.3
  155.9 0.2 convolution_dynamic-update-slice_fusion.34
  156.2 0.2 convolution_dynamic-update-slice_fusion.35
  156.4 0.2 convolution_dynamic-update-slice_fusion.36
  156.6 0.2 convolution_dynamic-update-slice_fusion.37
  156.8 0.2 convolution_dynamic-update-slice_fusion.38
  157.0 0.2 convolution_dynamic-update-slice_fusion.39
  157.3 0.2 convolution_dynamic-update-slice_fusion.40
  159.1 1.3 copy-done.27
  160.4 2.5 divide_convert_fusion.2
  162.9 2.9 fusion.213
  165.8 0.2 fusion.214
  166.1 0.2 convolution_add_fusion.13
  166.4 0.2 convolution_add_fusion.14
  166.6 0.2 convolution_add_fusion.15
  166.9 0.2 convolution_add_fusion.16
  167.1 0.2 convolution_add_fusion.17
  167.4 0.2 convolution_add_fusion.18
  167.6 0.2 fusion.215
  170.9 0.4 add_dynamic-update-slice_fusion.5
  171.3 1.0 copy-done.3
  172.3 1.1 slice.395
  173.5 1.0 slice.460
  174.5 1.3 collective-permute-start.2
  175.8 1.3 collective-permute-start.3
  177.1 0.8 fusion.63
  178.0 124.6 %psum.7 = f32[1024]{0:T(1024)S(1)} all-reduce(f32[1024]{0:T(1024)S(1)} %bitcast.480), channel_id=1, replica_groups=mesh['ctx'=16,'dp'=64] {'ctx','dp'}, use_global_device_ids=true, to_apply=%region_6.7 | all-reduce | flops 1024 | bytes 8192 | tf_op jit(solution)/shard_map/psum | solution.py:183
  302.6 0.6 dynamic_slice.90
  303.2 1.2 add_dynamic-update-slice_fusion.2
  304.4 0.7 copy-done.28
  (168 shorter events, 9.9 us)
Async XLA Ops:
  0.6 135.5 %copy-start.25 = (bf16[1,1024,128]{2,1,0:T(8,128)(2,1)S(1)}, bf16[1,1024,128]{2,1,0:T(8,128)(2,1)}, u32[]{:S(2)}) copy-start(bf16[1,1024,128]{2,1,0:T(8,128)(2,1)} %param.14) | copy-start | bytes 786436
  0.6 135.5 %copy-start.26 = (bf16[1,1024,128]{2,1,0:T(8,128)(2,1)S(1)}, bf16[1,1024,128]{2,1,0:T(8,128)(2,1)}, u32[]{:S(2)}) copy-start(bf16[1,1024,128]{2,1,0:T(8,128)(2,1)} %param.15) | copy-start | bytes 786436
  0.7 135.4 %copy-start.23 = (bf16[1,1024,128]{2,1,0:T(8,128)(2,1)S(1)}, bf16[1,1024,128]{2,1,0:T(8,128)(2,1)}, u32[]{:S(2)}) copy-start(bf16[1,1024,128]{2,1,0:T(8,128)(2,1)} %param.13) | copy-start | bytes 786436
  1.7 134.4 %collective-permute-start = (bf16[1,896,128]{2,1,0:T(8,128)(2,1)S(1)}, bf16[1,896,128]{2,1,0:T(8,128)(2,1)S(1)}, u32[]{:S(2)}, u32[]{:S(2)}) collective-permute-start(bf16[1,896,128]{2,1,0:T(8,128)(2,1)S(1)} %slice.390), channel_id=1, source_target_pairs={{0,64},{64,128},{128,192},{192,256},{256,320},{320,384},{384,448},... | collective-permute-start | bytes 688136 | tf_op jit(solution)/shard_map/ppermute | solution.py:16
  6.7 129.5 %collective-permute-start.1 = (bf16[1,896,128]{2,1,0:T(8,128)(2,1)S(1)}, bf16[1,896,128]{2,1,0:T(8,128)(2,1)S(1)}, u32[]{:S(2)}, u32[]{:S(2)}) collective-permute-start(bf16[1,896,128]{2,1,0:T(8,128)(2,1)S(1)} %slice.391), channel_id=1, source_target_pairs={{0,64},{64,128},{128,192},{192,256},{256,320},{320,384},{384,448},... | collective-permute-start | bytes 688136 | tf_op jit(solution)/shard_map/ppermute | solution.py:16
  136.1 2.1 copy-start
  138.3 1.9 copy-start.18
  138.3 2.2 copy-start.16
  138.3 2.4 copy-start.14
  138.3 2.6 copy-start.12
  138.3 2.8 copy-start.10
  138.3 3.0 copy-start.8
  138.3 3.2 %copy-start.6 = (bf16[1,512,128]{2,1,0:T(8,128)(2,1)}, bf16[1,512,128]{2,1,0:T(8,128)(2,1)S(1)}, u32[]{:S(2)}) copy-start(bf16[1,512,128]{2,1,0:T(8,128)(2,1)S(1)} %get-tuple-element.379) | copy-start | bytes 393220 | tf_op jit(solution)/shard_map/while
  138.3 3.4 %copy-start.4 = (bf16[1,512,128]{2,1,0:T(8,128)(2,1)}, bf16[1,512,128]{2,1,0:T(8,128)(2,1)S(1)}, u32[]{:S(2)}) copy-start(bf16[1,512,128]{2,1,0:T(8,128)(2,1)S(1)} %get-tuple-element.380) | copy-start | bytes 393220 | tf_op jit(solution)/shard_map/while
  140.2 1.8 copy-start.1
  142.0 1.3 copy-start.27
  145.8 2.9 copy-start.19
  145.8 3.2 %copy-start.17 = (bf16[1,512,128]{2,1,0:T(8,128)(2,1)S(1)}, bf16[1,512,128]{2,1,0:T(8,128)(2,1)}, u32[]{:S(2)}) copy-start(bf16[1,512,128]{2,1,0:T(8,128)(2,1)} %copy-done.16) | copy-start | bytes 393220 | tf_op jit(solution)/shard_map/while
  145.8 3.5 %copy-start.15 = (bf16[1,512,128]{2,1,0:T(8,128)(2,1)S(1)}, bf16[1,512,128]{2,1,0:T(8,128)(2,1)}, u32[]{:S(2)}) copy-start(bf16[1,512,128]{2,1,0:T(8,128)(2,1)} %copy-done.14) | copy-start | bytes 393220 | tf_op jit(solution)/shard_map/while
  145.8 3.7 %copy-start.13 = (bf16[1,512,128]{2,1,0:T(8,128)(2,1)S(1)}, bf16[1,512,128]{2,1,0:T(8,128)(2,1)}, u32[]{:S(2)}) copy-start(bf16[1,512,128]{2,1,0:T(8,128)(2,1)} %copy-done.12) | copy-start | bytes 393220 | tf_op jit(solution)/shard_map/while
  148.8 1.1 copy-start.11
  148.8 1.3 copy-start.9
  149.0 1.3 copy-start.7
  149.3 1.3 copy-start.5
  149.3 1.3 copy-start.20
  150.8 1.5 copy-start.21
  152.3 1.5 copy-start.2
  154.3 1.0 copy-start.3
  155.3 1.9 copy-start.18
  155.3 2.2 copy-start.16
  155.3 2.4 copy-start.14
  155.3 2.6 copy-start.12
  155.4 2.8 copy-start.10
  155.4 3.0 copy-start.8
  155.4 3.2 %copy-start.6 = (bf16[1,512,128]{2,1,0:T(8,128)(2,1)}, bf16[1,512,128]{2,1,0:T(8,128)(2,1)S(1)}, u32[]{:S(2)}) copy-start(bf16[1,512,128]{2,1,0:T(8,128)(2,1)S(1)} %get-tuple-element.379) | copy-start | bytes 393220 | tf_op jit(solution)/shard_map/while
  155.4 3.5 %copy-start.4 = (bf16[1,512,128]{2,1,0:T(8,128)(2,1)}, bf16[1,512,128]{2,1,0:T(8,128)(2,1)S(1)}, u32[]{:S(2)}) copy-start(bf16[1,512,128]{2,1,0:T(8,128)(2,1)S(1)} %get-tuple-element.380) | copy-start | bytes 393220 | tf_op jit(solution)/shard_map/while
  157.2 1.8 copy-start.1
  159.1 1.3 copy-start.27
  162.9 2.9 copy-start.19
  162.9 3.2 %copy-start.17 = (bf16[1,512,128]{2,1,0:T(8,128)(2,1)S(1)}, bf16[1,512,128]{2,1,0:T(8,128)(2,1)}, u32[]{:S(2)}) copy-start(bf16[1,512,128]{2,1,0:T(8,128)(2,1)} %copy-done.16) | copy-start | bytes 393220 | tf_op jit(solution)/shard_map/while
  162.9 3.5 %copy-start.15 = (bf16[1,512,128]{2,1,0:T(8,128)(2,1)S(1)}, bf16[1,512,128]{2,1,0:T(8,128)(2,1)}, u32[]{:S(2)}) copy-start(bf16[1,512,128]{2,1,0:T(8,128)(2,1)} %copy-done.14) | copy-start | bytes 393220 | tf_op jit(solution)/shard_map/while
  162.9 3.7 %copy-start.13 = (bf16[1,512,128]{2,1,0:T(8,128)(2,1)S(1)}, bf16[1,512,128]{2,1,0:T(8,128)(2,1)}, u32[]{:S(2)}) copy-start(bf16[1,512,128]{2,1,0:T(8,128)(2,1)} %copy-done.12) | copy-start | bytes 393220 | tf_op jit(solution)/shard_map/while
  165.8 1.1 copy-start.11
  165.8 1.3 copy-start.9
  166.1 1.3 copy-start.7
  166.3 1.3 copy-start.5
  166.3 1.3 copy-start.20
  167.9 1.5 copy-start.21
  169.4 1.5 copy-start.2
  171.3 1.0 copy-start.3
  172.3 4.8 %copy-start.22 = (f32[1,8,128,128]{3,2,1,0:T(8,128)S(1)}, f32[1,8,128,128]{3,2,1,0:T(8,128)}, u32[]{:S(2)}) copy-start(f32[1,8,128,128]{3,2,1,0:T(8,128)} %get-tuple-element.251) | copy-start | bytes 1572868
  172.3 4.9 %copy-start.24 = (bf16[1,1024,128]{2,1,0:T(8,128)(2,1)S(1)}, bf16[1,1024,128]{2,1,0:T(8,128)(2,1)}, u32[]{:S(2)}) copy-start(bf16[1,1024,128]{2,1,0:T(8,128)(2,1)} %param.13) | copy-start | bytes 786436
  174.5 128.6 %collective-permute-start.2 = (bf16[1,896,128]{2,1,0:T(8,128)(2,1)S(1)}, bf16[1,896,128]{2,1,0:T(8,128)(2,1)S(1)}, u32[]{:S(2)}, u32[]{:S(2)}) collective-permute-start(bf16[1,896,128]{2,1,0:T(8,128)(2,1)S(1)} %slice.461), channel_id=1, source_target_pairs={{64,0},{128,64},{192,128},{256,192},{320,256},{384,320},{448,384},... | collective-permute-start | bytes 688136 | tf_op jit(solution)/shard_map/ppermute | solution.py:16
  175.8 127.4 %collective-permute-start.3 = (bf16[1,896,128]{2,1,0:T(8,128)(2,1)S(1)}, bf16[1,896,128]{2,1,0:T(8,128)(2,1)S(1)}, u32[]{:S(2)}, u32[]{:S(2)}) collective-permute-start(bf16[1,896,128]{2,1,0:T(8,128)(2,1)S(1)} %slice.460), channel_id=1, source_target_pairs={{64,0},{128,64},{192,128},{256,192},{320,256},{384,320},{448,384},... | collective-permute-start | bytes 688136 | tf_op jit(solution)/shard_map/ppermute | solution.py:16
  303.2 1.2 copy-start.29
  304.4 0.7 copy-start.28
where the time goes:
time: 306 us; the launch traced here: 305 us
  blocking collectives  243 us (79%)
  other arithmetic  18.1 us (6%)
  matrix products  16.2 us (5%)
  local copies, waits for them, and re-layouts  14.7 us (5%)
  starting transfers between devices  9.83 us (3%)
    psum x1, blocking collectives, on_device(): everything = lax.psum(gain_table, ('ctx', 'dp'))  125 us
    unnamed x1, blocking collectives  119 us
    ppermute x4, starting transfers between devices, from_behind(): return lax.ppermute(value, axis, pairs)  9.83 us
    dot_general x32, matrix products, block_scores(): jnp.einsum('bnqd,bnkd->bnqk', left_rows, right_rows, preferred_element_ty...  6.73 us
  transfers between devices with their start and end apart: 4, of which 0 were waited for; matrix products, arithmetic and copies ran while one was open for 3% of the time, Pallas kernels for 0%

commit v1 on v0

v1 whole, which is shorter than its diff:
```python
import functools
import math

import jax
import jax.numpy as jnp
from jax import lax
from jax.experimental import pallas as pl
from jax.experimental.pallas import tpu as pltpu
from jax.sharding import PartitionSpec as P

HEADS = 8
BLK = 128
WBLK = 8
HALO = (WBLK - 1) * BLK
STEP = 2 * BLK
PIECE = HALO // 4
MESH = pl.DeviceIdType.MESH
NEG = -1e30


def send(source, target, send_sem, recv_sem, device):
    return pltpu.make_async_remote_copy(
        src_ref=source,
        dst_ref=target,
        send_sem=send_sem,
        recv_sem=recv_sem,
        device_id=device,
        device_id_type=MESH,
    )


def body(
    n_ctx,
    q_hbm, k_hbm, v_hbm, g_hbm, share_ref, doc_hbm, win_hbm,
    dq_ref, dk_ref, dv_ref, gg_ref,
    q_ref, go_ref, k_ext, v_ext, k_t, scaled, doc_ref, win_ref, low_ref,
    s_scr, p_scr, dp_scr, ds_scr, dk_acc, dv_acc,
    dk_out, dv_out, dk_in, dv_in,
    gain_ref, gain_row, gain_in, part_row, part_in, head_row, head_in, part_acc,
    load_sem, halo_send, halo_recv, back_send, back_recv,
    gain_send, gain_recv, part_send, part_recv, head_send, head_recv,
):
    tok = q_ref.shape[0]
    width = q_ref.shape[1]
    groups = tok // STEP
    window = STEP + HALO
    kblocks = window // BLK
    score_scale = 1.0 / math.sqrt(width)
    exp_scale = score_scale * math.log2(math.e)
    c = lax.axis_index("ctx")
    d = lax.axis_index("dp")
    row = d // HEADS
    mine = d % HEADS
    diagonal = row == mine

    barrier = pltpu.get_barrier_semaphore()
    for hop in range(1, n_ctx):
        pl.semaphore_signal(
            barrier, inc=1, device_id={"ctx": (c + hop) % n_ctx}, device_id_type=MESH
        )
    for other in range(HEADS):
        user = row + HEADS * other
        owner = HEADS * mine + other

        @pl.when(user != d)
        def _():
            pl.semaphore_signal(barrier, inc=1, device_id={"dp": user}, device_id_type=MESH)

        @pl.when(owner != d)
        def _():
            pl.semaphore_signal(barrier, inc=1, device_id={"dp": owner}, device_id_type=MESH)

    first_row = pl.multiple_of(c * tok, tok)
    loads = [
        pltpu.make_async_copy(k_hbm, k_ext.at[pl.ds(HALO, tok)], load_sem.at[0]),
        pltpu.make_async_copy(v_hbm, v_ext.at[pl.ds(HALO, tok)], load_sem.at[1]),
        pltpu.make_async_copy(q_hbm, q_ref, load_sem.at[2]),
        pltpu.make_async_copy(g_hbm, go_ref, load_sem.at[3]),
        pltpu.make_async_copy(doc_hbm.at[:, pl.ds(first_row, tok)], doc_ref, load_sem.at[4]),
        pltpu.make_async_copy(win_hbm.at[:, pl.ds(first_row, tok)], win_ref, load_sem.at[5]),
    ]
    gain_ref[...] = jnp.zeros_like(gain_ref)
    for load in loads:
        load.start()

    @pl.when(c == 0)
    def _():
        k_ext[pl.ds(0, HALO)] = jnp.zeros((HALO, width), k_ext.dtype)
        v_ext[pl.ds(0, HALO)] = jnp.zeros((HALO, width), v_ext.dtype)

    dk_acc[...] = jnp.zeros_like(dk_acc)
    dv_acc[...] = jnp.zeros_like(dv_acc)
    part_acc[...] = jnp.zeros_like(part_acc)

    gain_ref[:, 0 : share_ref.shape[1]] = share_ref[...]
    gain_row[...] = pltpu.roll(gain_ref[...], 16 * mine, 1)

    @pl.when(diagonal)
    def _():
        pl.semaphore_wait(barrier, n_ctx - 1 + 2 * (HEADS - 1))

    @pl.when(jnp.logical_not(diagonal))
    def _():
        pl.semaphore_wait(barrier, n_ctx - 1 + 2 * HEADS)

    def gain_copy(target, slot):
        return send(gain_row, gain_in.at[mine], gain_send.at[slot], gain_recv.at[mine], {"dp": target})

    def halo_copy(which, piece, source, target):
        return send(
            source.at[pl.ds(tok - HALO + piece * PIECE, PIECE)],
            target.at[pl.ds(piece * PIECE, PIECE)],
            halo_send.at[which, piece],
            halo_recv.at[which, piece],
            {"ctx": c + 1},
        )

    for other in range(HEADS):
        user = row + HEADS * other

        @pl.when(user != d)
        def _():
            gain_copy(user, other).start()

        @pl.when(user == d)
        def _():
            gain_in[mine] = gain_row[pl.ds(0, 1)]

    @pl.when(c < n_ctx - 1)
    def _():
        for piece in (3, 2, 1, 0):
            halo_copy(0, piece, k_hbm, k_ext).start()
        for piece in (3, 2, 1, 0):
            halo_copy(1, piece, v_hbm, v_ext).start()

    loads[4].wait()
    loads[5].wait()
    low_ref[...] = jnp.maximum(doc_ref[...], win_ref[...]) - (c * tok - HALO)
    loads[0].wait()
    for block in range(WBLK - 1, WBLK - 1 + tok // BLK):
        k_t[:, pl.ds(block * BLK, BLK)] = k_ext[pl.ds(block * BLK, BLK)].T
    loads[1].wait()
    loads[2].wait()
    loads[3].wait()

    for other in range(HEADS):
        owner = HEADS * mine + other

        @pl.when(owner != d)
        def _():
            send(
                gain_row, gain_in.at[other], gain_send.at[0], gain_recv.at[other], {"dp": owner}
            ).wait_recv()

    gain_all = gain_in[0]
    for other in range(1, HEADS):
        gain_all = gain_all + gain_in[other]
    scaled[...] = (q_ref[...].astype(jnp.float32) * gain_all).astype(scaled.dtype)

    seq = row

    def halo_arrives(which, group, source, target):
        @pl.when(c > 0)
        def _():
            halo_copy(which, group, source, target).wait_recv()

    def dot_nt(left, right):
        return lax.dot_general(
            left, right, (((1,), (1,)), ((), ())), preferred_element_type=jnp.float32
        )

    def softmax_step(step, carry):
        group = groups - 1 - step
        base = pl.multiple_of(group * STEP, STEP)
        halo_arrives(0, group, k_hbm, k_ext)
        query = scaled[pl.ds(base, STEP)]
        lower = low_ref[pl.ds(seq, 1), pl.ds(base, STEP)] - base
        highest = jnp.full((8, STEP), NEG, jnp.float32)
        for kb in range(kblocks):
            scores = dot_nt(k_ext[pl.ds(base + kb * BLK, BLK)], query)
            key_row = lax.broadcasted_iota(jnp.int32, (BLK, STEP), 0) + kb * BLK
            seen = key_row >= lower
            if kb >= WBLK - 1:
                seen = seen & (key_row - HALO <= lax.broadcasted_iota(jnp.int32, (BLK, STEP), 1))
            scores = jnp.where(seen, scores, NEG)
            s_scr[pl.ds(kb * BLK, BLK)] = scores
            highest = jnp.maximum(highest, jnp.max(scores.reshape(BLK // 8, 8, STEP), axis=0))
        highest = jnp.max(highest, axis=0, keepdims=True) * exp_scale
        total = jnp.zeros((8, STEP), jnp.float32)
        for kb in range(kblocks):
            weights = jnp.exp2(s_scr[pl.ds(kb * BLK, BLK)] * exp_scale - highest)
            s_scr[pl.ds(kb * BLK, BLK)] = weights
            total = total + jnp.sum(weights.reshape(BLK // 8, 8, STEP), axis=0)
        inverse = 1.0 / jnp.sum(total, axis=0, keepdims=True)
        for kb in range(kblocks):
            probs = (s_scr[pl.ds(kb * BLK, BLK)] * inverse).astype(p_scr.dtype)
            p_scr[group, pl.ds(kb * BLK, BLK)] = probs
        dv_acc[pl.ds(base, window)] += jnp.dot(
            p_scr[group], go_ref[pl.ds(base, STEP)], preferred_element_type=jnp.float32
        )
        return carry

    lax.fori_loop(0, groups, softmax_step, 0)

    back_dv = send(dv_out, dv_in, back_send.at[0], back_recv.at[0], {"ctx": c - 1})
    back_dk = send(dk_out, dk_in, back_send.at[1], back_recv.at[1], {"ctx": c - 1})

    dv_out[...] = dv_acc[pl.ds(0, HALO)].astype(dv_out.dtype)

    @pl.when(c > 0)
    def _():
        back_dv.start()

    for block in range(WBLK - 1):
        k_t[:, pl.ds(block * BLK, BLK)] = k_ext[pl.ds(block * BLK, BLK)].T

    def grad_step(step, carry):
        group = groups - 1 - step
        base = pl.multiple_of(group * STEP, STEP)
        halo_arrives(1, group, v_hbm, v_ext)
        grad = go_ref[pl.ds(base, STEP)]
        delta = jnp.zeros((8, STEP), jnp.float32)
        for kb in range(kblocks):
            prob_grad = dot_nt(v_ext[pl.ds(base + kb * BLK, BLK)], grad)
            dp_scr[pl.ds(kb * BLK, BLK)] = prob_grad
            terms = prob_grad * p_scr[group, pl.ds(kb * BLK, BLK)].astype(jnp.float32)
            delta = delta + jnp.sum(terms.reshape(BLK // 8, 8, STEP), axis=0)
        delta = jnp.sum(delta, axis=0, keepdims=True)
        for kb in range(kblocks):
            probs = p_scr[group, pl.ds(kb * BLK, BLK)].astype(jnp.float32)
            ds_scr[pl.ds(kb * BLK, BLK)] = (
                probs * (dp_scr[pl.ds(kb * BLK, BLK)] - delta)
            ).astype(ds_scr.dtype)
        score_grad = ds_scr[...]
        mixed_t = jnp.dot(
            k_t[:, pl.ds(base, window)], score_grad, preferred_element_type=jnp.float32
        )
        mixed = mixed_t.T * score_scale
        dq_ref[pl.ds(base, STEP)] = (mixed * gain_all).astype(dq_ref.dtype)
        terms = mixed * q_ref[pl.ds(base, STEP)].astype(jnp.float32)
        part_acc[...] += jnp.sum(terms.reshape(STEP // 8, 8, width), axis=0)
        dk_acc[pl.ds(base, window)] += jnp.dot(
            score_grad, scaled[pl.ds(base, STEP)], preferred_element_type=jnp.float32
        )
        return carry

    lax.fori_loop(0, groups, grad_step, 0)

    part_row[...] = jnp.sum(part_acc[...], axis=0, keepdims=True)

    def part_copy(hop):
        return send(
            part_row, part_in.at[hop], part_send.at[hop], part_recv.at[hop], {"ctx": (c + hop) % n_ctx}
        )

    for hop in range(1, n_ctx):
        part_copy(hop).start()
    dk_out[...] = (dk_acc[pl.ds(0, HALO)] * score_scale).astype(dk_out.dtype)

    @pl.when(c > 0)
    def _():
        back_dk.start()

    own_dk = dk_acc[pl.ds(HALO, tok)] * score_scale
    dk_acc[pl.ds(HALO, tok)] = own_dk
    dk_ref[...] = own_dk.astype(dk_ref.dtype)

    for hop in range(1, n_ctx):
        part_copy(hop).wait()
    across = part_row[...]
    for hop in range(1, n_ctx):
        across = across + part_in[hop]
    head_row[...] = across

    def head_copy(target, slot):
        return send(head_row, head_in.at[row], head_send.at[slot], head_recv.at[row], {"dp": target})

    for other in range(HEADS):
        owner = HEADS * mine + other

        @pl.when(owner != d)
        def _():
            head_copy(owner, other).start()

        @pl.when(owner == d)
        def _():
            head_in[row] = head_row[...]

    @pl.when(c < n_ctx - 1)
    def _():
        back_dv.wait_recv()

    dv_ref[...] = dv_acc[pl.ds(HALO, tok)].astype(dv_ref.dtype)

    @pl.when(c < n_ctx - 1)
    def _():
        dv_ref[pl.ds(tok - HALO, HALO)] = (
            dv_acc[pl.ds(tok, HALO)] + dv_in[...].astype(jnp.float32)
        ).astype(dv_ref.dtype)
        back_dk.wait_recv()
        dk_ref[pl.ds(tok - HALO, HALO)] = (
            dk_acc[pl.ds(tok, HALO)] + dk_in[...].astype(jnp.float32)
        ).astype(dk_ref.dtype)

    for other in range(HEADS):
        user = row + HEADS * other

        @pl.when(user != d)
        def _():
            send(
                head_row, head_in.at[other], head_send.at[0], head_recv.at[other], {"dp": user}
            ).wait_recv()

    whole = head_in[0]
    for other in range(1, HEADS):
        whole = whole + head_in[other]
    whole = pltpu.roll(jnp.broadcast_to(whole, (8, width)), (width - 16 * mine) % width, 1)
    gg_ref[...] = whole[0:1, 0 : gg_ref.shape[1]]

    for other in range(HEADS):
        user = row + HEADS * other
        owner = HEADS * mine + other

        @pl.when(user != d)
        def _():
            gain_copy(user, other).wait_send()

        @pl.when(owner != d)
        def _():
            head_copy(owner, other).wait_send()

    @pl.when(c < n_ctx - 1)
    def _():
        for piece in range(4):
            halo_copy(0, piece, k_hbm, k_ext).wait_send()
            halo_copy(1, piece, v_hbm, v_ext).wait_send()

    @pl.when(c > 0)
    def _():
        back_dv.wait_send()
        back_dk.wait_send()


def on_device(queries, keys, values, grad_out, gain, doc_start, win_start):
    _, tok, width = queries.shape
    n_ctx = lax.axis_size("ctx")
    seqs = doc_start.shape[0]
    share = gain.shape[0]
    window = STEP + HALO
    groups = tok // STEP
    wide = (HALO + tok, width)
    hbm = pl.BlockSpec(memory_space=pl.ANY)
    vmem = pl.BlockSpec(memory_space=pltpu.VMEM)
    dma = pltpu.SemaphoreType.DMA


    grads = pl.pallas_call(
        functools.partial(body, n_ctx),
        out_shape=[jax.ShapeDtypeStruct((tok, width), jnp.bfloat16)] * 3
        + [jax.ShapeDtypeStruct((1, share), jnp.float32)],
        in_specs=[hbm] * 4 + [vmem] + [hbm] * 2,
        out_specs=[vmem] * 4,
        scratch_shapes=[
            pltpu.VMEM((tok, width), jnp.bfloat16),
            pltpu.VMEM((tok, width), jnp.bfloat16),
            pltpu.VMEM(wide, jnp.bfloat16),
            pltpu.VMEM(wide, jnp.bfloat16),
            pltpu.VMEM((width, HALO + tok), jnp.bfloat16),
            pltpu.VMEM((tok, width), jnp.bfloat16),
            pltpu.VMEM((seqs, tok), jnp.int32),
            pltpu.VMEM((seqs, tok), jnp.int32),
            pltpu.VMEM((seqs, tok), jnp.int32),
            pltpu.VMEM((window, STEP), jnp.float32),
            pltpu.VMEM((groups, window, STEP), jnp.bfloat16),
            pltpu.VMEM((window, STEP), jnp.float32),
            pltpu.VMEM((window, STEP), jnp.bfloat16),
            pltpu.VMEM(wide, jnp.float32),
            pltpu.VMEM(wide, jnp.float32),
            pltpu.VMEM((HALO, width), jnp.bfloat16),
            pltpu.VMEM((HALO, width), jnp.bfloat16),
            pltpu.VMEM((HALO, width), jnp.bfloat16),
            pltpu.VMEM((HALO, width), jnp.bfloat16),
            pltpu.VMEM((1, width), jnp.float32),
            pltpu.VMEM((1, width), jnp.float32),
            pltpu.VMEM((HEADS, 1, width), jnp.float32),
            pltpu.VMEM((1, width), jnp.float32),
            pltpu.VMEM((n_ctx, 1, width), jnp.float32),
            pltpu.VMEM((1, width), jnp.float32),
            pltpu.VMEM((HEADS, 1, width), jnp.float32),
            pltpu.VMEM((8, width), jnp.float32),
            dma((6,)),
            dma((2, 4)),
            dma((2, 4)),
            dma((2,)),
            dma((2,)),
            dma((HEADS,)),
            dma((HEADS,)),
            dma((n_ctx,)),
            dma((n_ctx,)),
            dma((HEADS,)),
            dma((HEADS,)),
        ],
        compiler_params=pltpu.CompilerParams(
            collective_id=0, has_side_effects=True, vmem_limit_bytes=60 << 20
        ),
    )(
        queries.reshape(tok, width),
        keys.reshape(tok, width),
        values.reshape(tok, width),
        grad_out.reshape(tok, width),
        gain.reshape(1, share),
        doc_start,
        win_start,
    )
    shape = (1, tok, width)
    return (
        grads[0].reshape(shape),
        grads[1].reshape(shape),
        grads[2].reshape(shape),
        grads[3].reshape(share),
    )


def solution(mesh):
    rows = P("dp", "ctx", None)
    return jax.shard_map(
        on_device,
        mesh=mesh,
        in_specs=(rows, rows, rows, rows, P("dp"), P(), P()),
        out_specs=(rows, rows, rows, P("dp")),
        check_vma=False,
    )
```

time: 306 us -> 58.6 us (0.19)
  blocking collectives: 243 us -> 0 us
  Pallas kernels: 0 us -> 53.8 us
  other arithmetic: 18.1 us -> 0 us
  matrix products: 16.2 us -> 0 us
  local copies, waits for them, and re-layouts: 14.7 us -> 3.98 us
  starting transfers between devices: 9.83 us -> 0 us
    psum x1 -> x0, blocking collectives: 125 us -> none  [on_device(): everything = lax.psum(gain_table, ('ctx', 'dp'))]
    unnamed x1 -> x0, blocking collectives: 119 us -> none
    pallas_call x0 -> x1, Pallas kernels: none -> 53.8 us  [on_device(): pl.pallas_call(functools.partial(body, n_ctx), out_shape=[jax.ShapeDtypeS...]
    dot_general x80 -> x0, matrix products: 16.2 us -> none  [the longest x32 6.73 us: block_scores(): jnp.einsum('bnqd,bnkd->bnqk', left_rows, right_rows, preferred_element_ty...]
    ppermute x4 -> x0, starting transfers between devices: 9.83 us -> none  [from_behind(): return lax.ppermute(value, axis, pairs)]
    sub x2 -> x0, other arithmetic: 5.78 us -> none  [band_terms(): prob_grad - row_delta]
    div x2 -> x0, other arithmetic: 4.93 us -> none  [band_terms(): weights / jnp.sum(weights, axis=-1, keepdims=True)]
    while x88 -> x0, local copies, waits for them, and re-layouts: 4.73 us -> none
  transfers between devices with their start and end apart: 4 -> 0, of which waited for: 0 -> 0; matrix products, arithmetic and copies ran while one was open for 3% -> 0% of each run, Pallas kernels for 0% -> 0%
where the time goes in v1:
time: 58.6 us; the launch traced here: 58.4 us
  Pallas kernels  53.8 us (92%)
  local copies, waits for them, and re-layouts  3.98 us (7%)
  between operations  0.65 us (1%)
    pallas_call x1, Pallas kernels, on_device(): pl.pallas_call(functools.partial(body, n_ctx), out_shape=[jax.ShapeDtypeS...  53.8 us
    unnamed x10, local copies, waits for them, and re-layouts  3.98 us

profile of v1, /device:TPU:1, one launch (start us, length us, event | category | flops | bytes accessed | tf_op | source)
XLA Modules:
  0.0 58.4 jit_solution(8742309652021433100)
XLA Ops:
  0.6 53.8 %shard_map.102 = (bf16[1024,128]{1,0:T(8,128)(2,1)}, bf16[1024,128]{1,0:T(8,128)(2,1)}, bf16[1024,128]{1,0:T(8,128)(2,1)}, f32[1,16]{1,0:T(1,128)}) custom-call(bf16[1024,128]{1,0:T(8,128)(2,1)} %bitcast.9, bf16[1024,128]{1,0:T(8,128)(2,1)} %bitcast.10, bf16[1024,128]{1,0:T(8,128)(2,1)} %bitcast.11, bf16[1024,128]{1,0:T(8,128)(2,1)} %bitcast.12, ...), custom_call_target="tpu_custom_call" | custom-call | tf_op jit(solution)/shard_map/pallas_call | solution.py:357
  54.4 0.0 copy-start.1
  54.4 1.7 %copy.15 = bf16[1,1024,128]{2,1,0:T(8,128)(2,1)} copy(bf16[1,1024,128]{2,1,0:T(8,128)(2,1)} %bitcast.15) | data formatting | bytes 524288
  56.1 0.0 copy-done.1
  56.1 0.0 copy-start
  56.1 0.7 %copy.16 = bf16[1,1024,128]{2,1,0:T(8,128)(2,1)} copy(bf16[1,1024,128]{2,1,0:T(8,128)(2,1)S(1)} %bitcast.14) | data formatting | bytes 524288
  56.8 0.3 copy-done
  57.2 0.0 copy-start.2
  57.2 0.7 %copy.17 = bf16[1,1024,128]{2,1,0:T(8,128)(2,1)} copy(bf16[1,1024,128]{2,1,0:T(8,128)(2,1)S(1)} %bitcast.13) | data formatting | bytes 524288
  57.9 0.0 copy-done.2
  57.9 0.5 copy.18
Async XLA Ops:
  54.4 1.7 %copy-start.1 = (bf16[1024,128]{1,0:T(8,128)(2,1)S(1)}, bf16[1024,128]{1,0:T(8,128)(2,1)}, u32[]{:S(2)}) copy-start(bf16[1024,128]{1,0:T(8,128)(2,1)} %get-tuple-element.9) | copy-start | bytes 786436
  56.1 1.0 %copy-start = (bf16[1024,128]{1,0:T(8,128)(2,1)S(1)}, bf16[1024,128]{1,0:T(8,128)(2,1)}, u32[]{:S(2)}) copy-start(bf16[1024,128]{1,0:T(8,128)(2,1)} %get-tuple-element.10) | copy-start | bytes 786436
  57.2 0.7 %copy-start.2 = (f32[1,16]{1,0:T(1,128)S(1)}, f32[1,16]{1,0:T(1,128)}, u32[]{:S(2)}) copy-start(f32[1,16]{1,0:T(1,128)} %get-tuple-element.11) | copy-start | bytes 196

commit v2 on v1

--- a/solution.py
+++ b/solution.py
@@ -36,9 +36,9 @@
     q_ref, go_ref, k_ext, v_ext, k_t, scaled, doc_ref, win_ref, low_ref,
     s_scr, p_scr, dp_scr, ds_scr, dk_acc, dv_acc,
     dk_out, dv_out, dk_in, dv_in,
-    gain_ref, gain_row, gain_in, part_row, part_in, head_row, head_in, part_acc,
+    gain_ref, gain_row, gain_in, gain_full, part_rows, part_in, head_row, head_in, part_acc,
     load_sem, halo_send, halo_recv, back_send, back_recv,
-    gain_send, gain_recv, part_send, part_recv, head_send, head_recv,
+    gain_send, gain_recv, relay_send, relay_recv, part_send, part_recv, head_send, head_recv, met, met_rows,
 ):
     tok = q_ref.shape[0]
     width = q_ref.shape[1]
@@ -53,22 +53,56 @@
     mine = d % HEADS
     diagonal = row == mine
 
+    root = HEADS * row + row
+    along = n_ctx // 2
+    y = c % along
+    y_base = c - y
+    far_x = (c + along) % n_ctx
+    y_peers = [y_base + (y + hop + along) % along for hop in (2, -2, 1, -1)]
+    at_end = (y == 0) | (y == along - 1)
+    half = HEADS // 2
+
+    def source_of(other):
+        near = jnp.where(other < mine, other + 1, mine)
+        late = jnp.where(other < half, mine, near)
+        early = jnp.where(other < half, mine, jnp.where(other < half + 2, half - 1, 0))
+        return jnp.where(mine >= half, late, early)
+
+    source = source_of(row)
+    asked = source < row
+    feeds = [(source_of(jnp.int32(t)) == row) & (row != t) for t in range(HEADS)]
+
     barrier = pltpu.get_barrier_semaphore()
-    for hop in range(1, n_ctx):
-        pl.semaphore_signal(
-            barrier, inc=1, device_id={"ctx": (c + hop) % n_ctx}, device_id_type=MESH
-        )
-    for other in range(HEADS):
-        user = row + HEADS * other
-        owner = HEADS * mine + other
-
-        @pl.when(user != d)
-        def _():
-            pl.semaphore_signal(barrier, inc=1, device_id={"dp": user}, device_id_type=MESH)
-
-        @pl.when(owner != d)
-        def _():
-            pl.semaphore_signal(barrier, inc=1, device_id={"dp": owner}, device_id_type=MESH)
+
+    def greet(device):
+        pl.semaphore_signal(barrier, inc=1, device_id=device, device_id_type=MESH)
+
+    @pl.when(c > 0)
+    def _():
+        greet({"ctx": c - 1})
+
+    @pl.when(at_end)
+    def _():
+        greet({"ctx": y_base + along - 1 - y})
+
+    @pl.when(c < along)
+    def _():
+        greet({"ctx": far_x})
+
+    @pl.when(diagonal)
+    def _():
+        for other in range(1, HEADS):
+            greet({"dp": HEADS * row + (row + other) % HEADS})
+
+    @pl.when(row < source)
+    def _():
+        greet({"dp": HEADS * source + mine})
+
+    for t in range(HEADS):
+
+        @pl.when(feeds[t] & (row < t))
+        def _():
+            greet({"dp": HEADS * t + mine})
 
     first_row = pl.multiple_of(c * tok, tok)
     loads = [
@@ -95,16 +129,9 @@
     gain_ref[:, 0 : share_ref.shape[1]] = share_ref[...]
     gain_row[...] = pltpu.roll(gain_ref[...], 16 * mine, 1)
 
-    @pl.when(diagonal)
-    def _():
-        pl.semaphore_wait(barrier, n_ctx - 1 + 2 * (HEADS - 1))
-
-    @pl.when(jnp.logical_not(diagonal))
-    def _():
-        pl.semaphore_wait(barrier, n_ctx - 1 + 2 * HEADS)
-
-    def gain_copy(target, slot):
-        return send(gain_row, gain_in.at[mine], gain_send.at[slot], gain_recv.at[mine], {"dp": target})
+    terms = [c < n_ctx - 1, at_end, c >= along, jnp.logical_not(diagonal), asked]
+    terms += [feeds[t] & (row > t) for t in range(HEADS)]
+    pl.semaphore_wait(barrier, sum(jnp.where(term, 1, 0) for term in terms))
 
     def halo_copy(which, piece, source, target):
         return send(
@@ -115,16 +142,13 @@
             {"ctx": c + 1},
         )
 
-    for other in range(HEADS):
-        user = row + HEADS * other
-
-        @pl.when(user != d)
-        def _():
-            gain_copy(user, other).start()
-
-        @pl.when(user == d)
-        def _():
-            gain_in[mine] = gain_row[pl.ds(0, 1)]
+    to_root = send(gain_row, gain_in.at[mine], gain_send.at[0], gain_recv.at[mine], {"dp": root})
+
+    def feed(t):
+        return send(
+            gain_full, gain_full, relay_send.at[t], relay_recv.at[0], {"dp": HEADS * t + mine}
+        )
+
 
     @pl.when(c < n_ctx - 1)
     def _():
@@ -132,6 +156,45 @@
             halo_copy(0, piece, k_hbm, k_ext).start()
         for piece in (3, 2, 1, 0):
             halo_copy(1, piece, v_hbm, v_ext).start()
+
+    @pl.when(jnp.logical_not(diagonal))
+    def _():
+        to_root.start()
+
+    @pl.when(asked)
+    def _():
+        pl.semaphore_signal(
+            met_rows.at[row], inc=1, device_id={"dp": HEADS * source + mine}, device_id_type=MESH
+        )
+
+    @pl.when(c >= along)
+    def _():
+        pl.semaphore_signal(met.at[2], inc=1, device_id={"ctx": far_x}, device_id_type=MESH)
+
+    @pl.when(diagonal)
+    def _():
+        total = gain_row[...]
+        for other in range(1, HEADS):
+            piece = (row + other) % HEADS
+            send(
+                gain_row, gain_in.at[piece], gain_send.at[0], gain_recv.at[piece], {"dp": HEADS * row + piece}
+            ).wait_recv()
+            total = total + gain_in[piece]
+        gain_full[...] = total
+
+    @pl.when(jnp.logical_not(diagonal))
+    def _():
+        feed(0).wait_recv()
+
+    for t in range(HEADS):
+
+        @pl.when(feeds[t] & (row < t))
+        def _():
+            pl.semaphore_wait(met_rows.at[t], 1)
+
+        @pl.when(feeds[t])
+        def _():
+            feed(t).start()
 
     loads[4].wait()
     loads[5].wait()
@@ -143,18 +206,7 @@
     loads[2].wait()
     loads[3].wait()
 
-    for other in range(HEADS):
-        owner = HEADS * mine + other
-
-        @pl.when(owner != d)
-        def _():
-            send(
-                gain_row, gain_in.at[other], gain_send.at[0], gain_recv.at[other], {"dp": owner}
-            ).wait_recv()
-
-    gain_all = gain_in[0]
-    for other in range(1, HEADS):
-        gain_all = gain_all + gain_in[other]
+    gain_all = gain_full[...]
     scaled[...] = (q_ref[...].astype(jnp.float32) * gain_all).astype(scaled.dtype)
 
     seq = row
@@ -169,48 +221,40 @@
             left, right, (((1,), (1,)), ((), ())), preferred_element_type=jnp.float32
         )
 
+    def chunk(at):
+        return pl.ds(at * BLK, BLK)
+
     def softmax_step(step, carry):
         group = groups - 1 - step
         base = pl.multiple_of(group * STEP, STEP)
         halo_arrives(0, group, k_hbm, k_ext)
-        query = scaled[pl.ds(base, STEP)]
+        s_scr[...] = dot_nt(k_ext[pl.ds(base, window)], scaled[pl.ds(base, STEP)])
         lower = low_ref[pl.ds(seq, 1), pl.ds(base, STEP)] - base
+        key_row = lax.broadcasted_iota(jnp.int32, (BLK, STEP), 0)
+        query_row = lax.broadcasted_iota(jnp.int32, (BLK, STEP), 1)
         highest = jnp.full((8, STEP), NEG, jnp.float32)
         for kb in range(kblocks):
-            scores = dot_nt(k_ext[pl.ds(base + kb * BLK, BLK)], query)
-            key_row = lax.broadcasted_iota(jnp.int32, (BLK, STEP), 0) + kb * BLK
-            seen = key_row >= lower
+            seen = key_row >= lower - kb * BLK
             if kb >= WBLK - 1:
-                seen = seen & (key_row - HALO <= lax.broadcasted_iota(jnp.int32, (BLK, STEP), 1))
-            scores = jnp.where(seen, scores, NEG)
-            s_scr[pl.ds(kb * BLK, BLK)] = scores
+                seen = seen & (key_row <= query_row + (HALO - kb * BLK))
+            scores = jnp.where(seen, s_scr[chunk(kb)], NEG)
+            s_scr[chunk(kb)] = scores
             highest = jnp.maximum(highest, jnp.max(scores.reshape(BLK // 8, 8, STEP), axis=0))
         highest = jnp.max(highest, axis=0, keepdims=True) * exp_scale
         total = jnp.zeros((8, STEP), jnp.float32)
         for kb in range(kblocks):
-            weights = jnp.exp2(s_scr[pl.ds(kb * BLK, BLK)] * exp_scale - highest)
-            s_scr[pl.ds(kb * BLK, BLK)] = weights
+            weights = jnp.exp2(s_scr[chunk(kb)] * exp_scale - highest)
+            s_scr[chunk(kb)] = weights
             total = total + jnp.sum(weights.reshape(BLK // 8, 8, STEP), axis=0)
         inverse = 1.0 / jnp.sum(total, axis=0, keepdims=True)
         for kb in range(kblocks):
-            probs = (s_scr[pl.ds(kb * BLK, BLK)] * inverse).astype(p_scr.dtype)
-            p_scr[group, pl.ds(kb * BLK, BLK)] = probs
-        dv_acc[pl.ds(base, window)] += jnp.dot(
-            p_scr[group], go_ref[pl.ds(base, STEP)], preferred_element_type=jnp.float32
-        )
+            p_scr[group, chunk(kb)] = (s_scr[chunk(kb)] * inverse).astype(p_scr.dtype)
         return carry
 
     lax.fori_loop(0, groups, softmax_step, 0)
 
-    back_dv = send(dv_out, dv_in, back_send.at[0], back_recv.at[0], {"ctx": c - 1})
-    back_dk = send(dk_out, dk_in, back_send.at[1], back_recv.at[1], {"ctx": c - 1})
-
-    dv_out[...] = dv_acc[pl.ds(0, HALO)].astype(dv_out.dtype)
-
-    @pl.when(c > 0)
-    def _():
-        back_dv.start()
-
+    pl.semaphore_signal(met.at[0], inc=1, device_id={"ctx": y_peers[2]}, device_id_type=MESH)
+    pl.semaphore_signal(met.at[1], inc=1, device_id={"ctx": y_peers[3]}, device_id_type=MESH)
     for block in range(WBLK - 1):
         k_t[:, pl.ds(block * BLK, BLK)] = k_ext[pl.ds(block * BLK, BLK)].T
 
@@ -218,59 +262,99 @@
         group = groups - 1 - step
         base = pl.multiple_of(group * STEP, STEP)
         halo_arrives(1, group, v_hbm, v_ext)
-        grad = go_ref[pl.ds(base, STEP)]
+        dp_scr[...] = dot_nt(v_ext[pl.ds(base, window)], go_ref[pl.ds(base, STEP)])
         delta = jnp.zeros((8, STEP), jnp.float32)
         for kb in range(kblocks):
-            prob_grad = dot_nt(v_ext[pl.ds(base + kb * BLK, BLK)], grad)
-            dp_scr[pl.ds(kb * BLK, BLK)] = prob_grad
-            terms = prob_grad * p_scr[group, pl.ds(kb * BLK, BLK)].astype(jnp.float32)
+            terms = dp_scr[chunk(kb)] * p_scr[group, chunk(kb)].astype(jnp.float32)
             delta = delta + jnp.sum(terms.reshape(BLK // 8, 8, STEP), axis=0)
         delta = jnp.sum(delta, axis=0, keepdims=True)
         for kb in range(kblocks):
-            probs = p_scr[group, pl.ds(kb * BLK, BLK)].astype(jnp.float32)
-            ds_scr[pl.ds(kb * BLK, BLK)] = (
-                probs * (dp_scr[pl.ds(kb * BLK, BLK)] - delta)
-            ).astype(ds_scr.dtype)
-        score_grad = ds_scr[...]
+            probs = p_scr[group, chunk(kb)].astype(jnp.float32)
+            ds_scr[group, chunk(kb)] = (probs * (dp_scr[chunk(kb)] - delta)).astype(ds_scr.dtype)
         mixed_t = jnp.dot(
-            k_t[:, pl.ds(base, window)], score_grad, preferred_element_type=jnp.float32
+            k_t[:, pl.ds(base, window)], ds_scr[group], preferred_element_type=jnp.float32
         )
         mixed = mixed_t.T * score_scale
         dq_ref[pl.ds(base, STEP)] = (mixed * gain_all).astype(dq_ref.dtype)
         terms = mixed * q_ref[pl.ds(base, STEP)].astype(jnp.float32)
         part_acc[...] += jnp.sum(terms.reshape(STEP // 8, 8, width), axis=0)
-        dk_acc[pl.ds(base, window)] += jnp.dot(
-            score_grad, scaled[pl.ds(base, STEP)], preferred_element_type=jnp.float32
-        )
         return carry
 
     lax.fori_loop(0, groups, grad_step, 0)
 
-    part_row[...] = jnp.sum(part_acc[...], axis=0, keepdims=True)
-
-    def part_copy(hop):
-        return send(
-            part_row, part_in.at[hop], part_send.at[hop], part_recv.at[hop], {"ctx": (c + hop) % n_ctx}
-        )
-
-    for hop in range(1, n_ctx):
-        part_copy(hop).start()
-    dk_out[...] = (dk_acc[pl.ds(0, HALO)] * score_scale).astype(dk_out.dtype)
-
-    @pl.when(c > 0)
-    def _():
-        back_dk.start()
-
+    back_dv = send(dv_out, dv_in, back_send.at[0], back_recv.at[0], {"ctx": c - 1})
+    back_dk = send(dk_out, dk_in, back_send.at[1], back_recv.at[1], {"ctx": c - 1})
+
+    def key_grads():
+        def step(group, carry):
+            base = pl.multiple_of(group * STEP, STEP)
+            dk_acc[pl.ds(base, window)] += jnp.dot(
+                ds_scr[group], scaled[pl.ds(base, STEP)], preferred_element_type=jnp.float32
+            )
+            return carry
+
+        lax.fori_loop(0, groups, step, 0)
+        dk_out[...] = (dk_acc[pl.ds(0, HALO)] * score_scale).astype(dk_out.dtype)
+
+        @pl.when(c > 0)
+        def _():
+            back_dk.start()
+
+    def value_grads():
+        def step(group, carry):
+            base = pl.multiple_of(group * STEP, STEP)
+            dv_acc[pl.ds(base, window)] += jnp.dot(
+                p_scr[group], go_ref[pl.ds(base, STEP)], preferred_element_type=jnp.float32
+            )
+            return carry
+
+        lax.fori_loop(0, groups, step, 0)
+        dv_out[...] = dv_acc[pl.ds(0, HALO)].astype(dv_out.dtype)
+
+        @pl.when(c > 0)
+        def _():
+            back_dv.start()
+
+    part_rows[0] = jnp.sum(part_acc[...], axis=0, keepdims=True)
+
+    def part_copy(source, slot, target):
+        return send(source, part_in.at[slot], part_send.at[slot], part_recv.at[slot], {"ctx": target})
+
+    over_x = part_copy(part_rows.at[0], 0, far_x)
+    over_y = [
+        part_copy(part_rows.at[1], 1 + at, peer) for at, peer in enumerate(y_peers)
+    ]
+    on_up = part_copy(part_in.at[3], 5, y_peers[0])
+    on_down = part_copy(part_rows.at[2], 6, y_peers[1])
+
+    @pl.when(c < along)
+    def _():
+        pl.semaphore_wait(met.at[2], 1)
+
+    over_x.start()
+    value_grads()
+    pl.semaphore_wait(met.at[0], 1)
+    pl.semaphore_wait(met.at[1], 1)
+    over_x.wait_recv()
+    part_rows[1] = part_rows[0] + part_in[0]
+    for copy in over_y:
+        copy.start()
+    key_grads()
     own_dk = dk_acc[pl.ds(HALO, tok)] * score_scale
     dk_acc[pl.ds(HALO, tok)] = own_dk
     dk_ref[...] = own_dk.astype(dk_ref.dtype)
-
-    for hop in range(1, n_ctx):
-        part_copy(hop).wait()
-    across = part_row[...]
-    for hop in range(1, n_ctx):
-        across = across + part_in[hop]
-    head_row[...] = across
+    dv_ref[...] = dv_acc[pl.ds(HALO, tok)].astype(dv_ref.dtype)
+    over_y[2].wait_recv()
+    on_up.start()
+    over_y[1].wait_recv()
+    over_y[3].wait_recv()
+    part_rows[2] = part_in[2] + part_in[4]
+    on_down.start()
+    over_y[0].wait_recv()
+    across = part_rows[1] + part_in[1] + part_in[2] + part_in[3] + part_in[4]
+    on_up.wait_recv()
+    on_down.wait_recv()
+    head_row[...] = across + part_in[5] + part_in[6]
 
     def head_copy(target, slot):
         return send(head_row, head_in.at[row], head_send.at[slot], head_recv.at[row], {"dp": target})
@@ -289,8 +373,6 @@
     @pl.when(c < n_ctx - 1)
     def _():
         back_dv.wait_recv()
-
-    dv_ref[...] = dv_acc[pl.ds(HALO, tok)].astype(dv_ref.dtype)
 
     @pl.when(c < n_ctx - 1)
     def _():
@@ -318,16 +400,24 @@
     gg_ref[...] = whole[0:1, 0 : gg_ref.shape[1]]
 
     for other in range(HEADS):
-        user = row + HEADS * other
         owner = HEADS * mine + other
 
-        @pl.when(user != d)
-        def _():
-            gain_copy(user, other).wait_send()
-
         @pl.when(owner != d)
         def _():
             head_copy(owner, other).wait_send()
+
+    for copy in [over_x, *over_y, on_up, on_down]:
+        copy.wait_send()
+
+    @pl.when(jnp.logical_not(diagonal))
+    def _():
+        to_root.wait_send()
+
+    for t in range(HEADS):
+
+        @pl.when(feeds[t])
+        def _():
+            feed(t).wait_send()
 
     @pl.when(c < n_ctx - 1)
     def _():
@@ -339,6 +429,25 @@
     def _():
         back_dv.wait_send()
         back_dk.wait_send()
+
+
+def deliver(*refs):
+    sources, targets, held, sems = refs[:4], refs[4:8], refs[8:12], refs[12]
+    loads = [
+        pltpu.make_async_copy(source, hold, sems.at[0, at])
+        for at, (source, hold) in enumerate(zip(sources, held))
+    ]
+    stores = [
+        pltpu.make_async_copy(hold, target, sems.at[1, at])
+        for at, (target, hold) in enumerate(zip(targets, held))
+    ]
+    for load in loads:
+        load.start()
+    for load, store in zip(loads, stores):
+        load.wait()
+        store.start()
+    for store in stores:
+        store.wait()
 
 
 def on_device(queries, keys, values, grad_out, gain, doc_start, win_start):
@@ -373,7 +482,7 @@
             pltpu.VMEM((window, STEP), jnp.float32),
             pltpu.VMEM((groups, window, STEP), jnp.bfloat16),
             pltpu.VMEM((window, STEP), jnp.float32),
-            pltpu.VMEM((window, STEP), jnp.bfloat16),
+            pltpu.VMEM((groups, window, STEP), jnp.bfloat16),
             pltpu.VMEM(wide, jnp.float32),
             pltpu.VMEM(wide, jnp.float32),
             pltpu.VMEM((HALO, width), jnp.bfloat16),
@@ -384,7 +493,8 @@
             pltpu.VMEM((1, width), jnp.float32),
             pltpu.VMEM((HEADS, 1, width), jnp.float32),
             pltpu.VMEM((1, width), jnp.float32),
-            pltpu.VMEM((n_ctx, 1, width), jnp.float32),
+            pltpu.VMEM((3, 1, width), jnp.float32),
+            pltpu.VMEM((7, 1, width), jnp.float32),
             pltpu.VMEM((1, width), jnp.float32),
             pltpu.VMEM((HEADS, 1, width), jnp.float32),
             pltpu.VMEM((8, width), jnp.float32),
@@ -393,12 +503,16 @@
             dma((2, 4)),
             dma((2,)),
             dma((2,)),
+            dma((1,)),
             dma((HEADS,)),
             dma((HEADS,)),
-            dma((n_ctx,)),
-            dma((n_ctx,)),
+            dma((1,)),
+            dma((7,)),
+            dma((7,)),
             dma((HEADS,)),
             dma((HEADS,)),
+            pltpu.SemaphoreType.REGULAR((3,)),
+            pltpu.SemaphoreType.REGULAR((HEADS,)),
         ],
         compiler_params=pltpu.CompilerParams(
             collective_id=0, has_side_effects=True, vmem_limit_bytes=60 << 20
@@ -412,6 +526,14 @@
         doc_start,
         win_start,
     )
+    grads = pl.pallas_call(
+        deliver,
+        out_shape=[jax.ShapeDtypeStruct(grad.shape, grad.dtype) for grad in grads],
+        in_specs=[hbm] * 4,
+        out_specs=[hbm] * 4,
+        scratch_shapes=[pltpu.VMEM(grad.shape, grad.dtype) for grad in grads] + [dma((2, 4))],
+        compiler_params=pltpu.CompilerParams(vmem_limit_bytes=60 << 20),
+    )(*grads)
     shape = (1, tok, width)
     return (
         grads[0].reshape(shape),

time: 58.6 us -> 58.4 us (level)
  local copies, waits for them, and re-layouts: 3.98 us -> 0 us
  Pallas kernels: 53.8 us -> 57.6 us
    unnamed x10 -> x0, local copies, waits for them, and re-layouts: 3.98 us -> none
    pallas_call x1, Pallas kernels: 53.8 us -> 55.7 us  [on_device(): pl.pallas_call(functools.partial(body, n_ctx), out_shape=[jax.ShapeDtypeS...]
    pallas_call x0 -> x1, Pallas kernels: none -> 1.9 us  [on_device(): pl.pallas_call(deliver, out_shape=[jax.ShapeDtypeStruct(grad.shape, grad....]
where the time goes in v2:
time: 58.4 us; the launch traced here: 58.2 us
  Pallas kernels  57.6 us (99%)
  between operations  0.64 us (1%)
    pallas_call x1, Pallas kernels, on_device(): pl.pallas_call(functools.partial(body, n_ctx), out_shape=[jax.ShapeDtypeS...  55.7 us
    pallas_call x1, Pallas kernels, on_device(): pl.pallas_call(deliver, out_shape=[jax.ShapeDtypeStruct(grad.shape, grad....  1.9 us

profile of v2, /device:TPU:1, one launch (start us, length us, event | category | flops | bytes accessed | tf_op | source)
XLA Modules:
  0.0 58.2 jit_solution(18306168874992953981)
XLA Ops:
  0.6 55.7 %shard_map.102 = (bf16[1024,128]{1,0:T(8,128)(2,1)}, bf16[1024,128]{1,0:T(8,128)(2,1)}, bf16[1024,128]{1,0:T(8,128)(2,1)}, f32[1,16]{1,0:T(1,128)}) custom-call(bf16[1024,128]{1,0:T(8,128)(2,1)} %bitcast.9, bf16[1024,128]{1,0:T(8,128)(2,1)} %bitcast.10, bf16[1024,128]{1,0:T(8,128)(2,1)} %bitcast.11, bf16[1024,128]{1,0:T(8,128)(2,1)} %bitcast.12, ...), custom_call_target="tpu_custom_call" | custom-call | tf_op jit(solution)/shard_map/pallas_call | solution.py:466
  56.3 1.9 %shard_map.103 = (bf16[1024,128]{1,0:T(8,128)(2,1)}, bf16[1024,128]{1,0:T(8,128)(2,1)}, bf16[1024,128]{1,0:T(8,128)(2,1)}, f32[1,16]{1,0:T(1,128)}) custom-call(bf16[1024,128]{1,0:T(8,128)(2,1)} %get-tuple-element.12.refs_0_, bf16[1024,128]{1,0:T(8,128)(2,1)} %get-tuple-element.13.refs_1_, bf16[1024,128]{1,0:T(8,128)(2,1)} %get-tuple-element.14.refs_2_, ...), custom_call_target="tpu_custom_call" | custom-call | tf_op jit(solution)/shard_map/pallas_call | solution.py:529

commit v3 on v2

--- a/solution.py
+++ b/solution.py
@@ -150,6 +150,20 @@
         )
 
 
+    @pl.when(jnp.logical_not(diagonal))
+    def _():
+        to_root.start()
+
+    @pl.when(asked)
+    def _():
+        pl.semaphore_signal(
+            met_rows.at[row], inc=1, device_id={"dp": HEADS * source + mine}, device_id_type=MESH
+        )
+
+    @pl.when(c >= along)
+    def _():
+        pl.semaphore_signal(met.at[2], inc=1, device_id={"ctx": far_x}, device_id_type=MESH)
+
     @pl.when(c < n_ctx - 1)
     def _():
         for piece in (3, 2, 1, 0):
@@ -157,19 +171,7 @@
         for piece in (3, 2, 1, 0):
             halo_copy(1, piece, v_hbm, v_ext).start()
 
-    @pl.when(jnp.logical_not(diagonal))
-    def _():
-        to_root.start()
-
-    @pl.when(asked)
-    def _():
-        pl.semaphore_signal(
-            met_rows.at[row], inc=1, device_id={"dp": HEADS * source + mine}, device_id_type=MESH
-        )
-
-    @pl.when(c >= along)
-    def _():
-        pl.semaphore_signal(met.at[2], inc=1, device_id={"ctx": far_x}, device_id_type=MESH)
+    hands_on = sum(jnp.where(feed_t, 1, 0) for feed_t in feeds) > 0
 
     @pl.when(diagonal)
     def _():
@@ -182,7 +184,7 @@
             total = total + gain_in[piece]
         gain_full[...] = total
 
-    @pl.when(jnp.logical_not(diagonal))
+    @pl.when(jnp.logical_not(diagonal) & hands_on)
     def _():
         feed(0).wait_recv()
 
@@ -206,8 +208,6 @@
     loads[2].wait()
     loads[3].wait()
 
-    gain_all = gain_full[...]
-    scaled[...] = (q_ref[...].astype(jnp.float32) * gain_all).astype(scaled.dtype)
 
     seq = row
 
@@ -224,10 +224,47 @@
     def chunk(at):
         return pl.ds(at * BLK, BLK)
 
-    def softmax_step(step, carry):
+    def chunk(at):
+        return pl.ds(at * BLK, BLK)
+
+    @pl.when(c > 0)
+    def _():
+        for piece in range(4):
+            halo_copy(0, piece, k_hbm, k_ext).wait_recv()
+
+    pl.semaphore_signal(met.at[0], inc=1, device_id={"ctx": y_peers[2]}, device_id_type=MESH)
+    pl.semaphore_signal(met.at[1], inc=1, device_id={"ctx": y_peers[3]}, device_id_type=MESH)
+    for block in range(WBLK - 1):
+        k_t[:, pl.ds(block * BLK, BLK)] = k_ext[pl.ds(block * BLK, BLK)].T
+
+    def prob_grad_step(step, carry):
         group = groups - 1 - step
         base = pl.multiple_of(group * STEP, STEP)
-        halo_arrives(0, group, k_hbm, k_ext)
+        halo_arrives(1, group, v_hbm, v_ext)
+        dp_scr[group] = dot_nt(v_ext[pl.ds(base, window)], go_ref[pl.ds(base, STEP)])
+        return carry
+
+    lax.fori_loop(0, groups, prob_grad_step, 0)
+
+    pl.semaphore_wait(met.at[0], 1)
+    pl.semaphore_wait(met.at[1], 1)
+
+    @pl.when(c < along)
+    def _():
+        pl.semaphore_wait(met.at[2], 1)
+
+    pl.semaphore_signal(met.at[3], inc=1, device_id={"ctx": far_x}, device_id_type=MESH)
+
+    @pl.when(jnp.logical_not(diagonal | hands_on))
+    def _():
+        feed(0).wait_recv()
+
+    gain_all = gain_full[...]
+    scaled[...] = (q_ref[...].astype(jnp.float32) * gain_all).astype(scaled.dtype)
+
+    def query_step(step, carry):
+        group = groups - 1 - step
+        base = pl.multiple_of(group * STEP, STEP)
         s_scr[...] = dot_nt(k_ext[pl.ds(base, window)], scaled[pl.ds(base, STEP)])
         lower = low_ref[pl.ds(seq, 1), pl.ds(base, STEP)] - base
         key_row = lax.broadcasted_iota(jnp.int32, (BLK, STEP), 0)
@@ -247,40 +284,28 @@
             s_scr[chunk(kb)] = weights
             total = total + jnp.sum(weights.reshape(BLK // 8, 8, STEP), axis=0)
         inverse = 1.0 / jnp.sum(total, axis=0, keepdims=True)
-        for kb in range(kblocks):
-            p_scr[group, chunk(kb)] = (s_scr[chunk(kb)] * inverse).astype(p_scr.dtype)
-        return carry
-
-    lax.fori_loop(0, groups, softmax_step, 0)
-
-    pl.semaphore_signal(met.at[0], inc=1, device_id={"ctx": y_peers[2]}, device_id_type=MESH)
-    pl.semaphore_signal(met.at[1], inc=1, device_id={"ctx": y_peers[3]}, device_id_type=MESH)
-    for block in range(WBLK - 1):
-        k_t[:, pl.ds(block * BLK, BLK)] = k_ext[pl.ds(block * BLK, BLK)].T
-
-    def grad_step(step, carry):
-        group = groups - 1 - step
-        base = pl.multiple_of(group * STEP, STEP)
-        halo_arrives(1, group, v_hbm, v_ext)
-        dp_scr[...] = dot_nt(v_ext[pl.ds(base, window)], go_ref[pl.ds(base, STEP)])
         delta = jnp.zeros((8, STEP), jnp.float32)
         for kb in range(kblocks):
-            terms = dp_scr[chunk(kb)] * p_scr[group, chunk(kb)].astype(jnp.float32)
-            delta = delta + jnp.sum(terms.reshape(BLK // 8, 8, STEP), axis=0)
+            probs = (s_scr[chunk(kb)] * inverse).astype(p_scr.dtype)
+            p_scr[group, chunk(kb)] = probs
+            products = dp_scr[group, chunk(kb)] * probs.astype(jnp.float32)
+            delta = delta + jnp.sum(products.reshape(BLK // 8, 8, STEP), axis=0)
         delta = jnp.sum(delta, axis=0, keepdims=True)
         for kb in range(kblocks):
             probs = p_scr[group, chunk(kb)].astype(jnp.float32)
-            ds_scr[group, chunk(kb)] = (probs * (dp_scr[chunk(kb)] - delta)).astype(ds_scr.dtype)
+            ds_scr[group, chunk(kb)] = (probs * (dp_scr[group, chunk(kb)] - delta)).astype(
+                ds_scr.dtype
+            )
         mixed_t = jnp.dot(
             k_t[:, pl.ds(base, window)], ds_scr[group], preferred_element_type=jnp.float32
         )
         mixed = mixed_t.T * score_scale
         dq_ref[pl.ds(base, STEP)] = (mixed * gain_all).astype(dq_ref.dtype)
-        terms = mixed * q_ref[pl.ds(base, STEP)].astype(jnp.float32)
-        part_acc[...] += jnp.sum(terms.reshape(STEP // 8, 8, width), axis=0)
+        products = mixed * q_ref[pl.ds(base, STEP)].astype(jnp.float32)
+        part_acc[...] += jnp.sum(products.reshape(STEP // 8, 8, width), axis=0)
         return carry
 
-    lax.fori_loop(0, groups, grad_step, 0)
+    lax.fori_loop(0, groups, query_step, 0, unroll=True)
 
     back_dv = send(dv_out, dv_in, back_send.at[0], back_recv.at[0], {"ctx": c - 1})
     back_dk = send(dk_out, dk_in, back_send.at[1], back_recv.at[1], {"ctx": c - 1})
@@ -320,41 +345,34 @@
     def part_copy(source, slot, target):
         return send(source, part_in.at[slot], part_send.at[slot], part_recv.at[slot], {"ctx": target})
 
-    over_x = part_copy(part_rows.at[0], 0, far_x)
-    over_y = [
-        part_copy(part_rows.at[1], 1 + at, peer) for at, peer in enumerate(y_peers)
-    ]
-    on_up = part_copy(part_in.at[3], 5, y_peers[0])
-    on_down = part_copy(part_rows.at[2], 6, y_peers[1])
-
-    @pl.when(c < along)
-    def _():
-        pl.semaphore_wait(met.at[2], 1)
-
-    over_x.start()
+    x_peers = [(peer + along) % n_ctx for peer in y_peers]
+    targets = x_peers + y_peers + [far_x]
+    spread = [part_copy(part_rows.at[0], at, target) for at, target in enumerate(targets)]
+    on_up = part_copy(part_rows.at[1], 9, y_peers[0])
+    on_down = part_copy(part_rows.at[2], 10, y_peers[1])
+    pl.semaphore_wait(met.at[3], 1)
+    for copy in spread:
+        copy.start()
     value_grads()
-    pl.semaphore_wait(met.at[0], 1)
-    pl.semaphore_wait(met.at[1], 1)
-    over_x.wait_recv()
-    part_rows[1] = part_rows[0] + part_in[0]
-    for copy in over_y:
-        copy.start()
     key_grads()
+    spread[2].wait_recv()
+    spread[6].wait_recv()
+    part_rows[1] = part_in[2] + part_in[6]
+    on_up.start()
+    for at in (1, 3, 5, 7):
+        spread[at].wait_recv()
+    part_rows[2] = part_in[1] + part_in[3] + part_in[5] + part_in[7]
+    on_down.start()
     own_dk = dk_acc[pl.ds(HALO, tok)] * score_scale
     dk_acc[pl.ds(HALO, tok)] = own_dk
     dk_ref[...] = own_dk.astype(dk_ref.dtype)
     dv_ref[...] = dv_acc[pl.ds(HALO, tok)].astype(dv_ref.dtype)
-    over_y[2].wait_recv()
-    on_up.start()
-    over_y[1].wait_recv()
-    over_y[3].wait_recv()
-    part_rows[2] = part_in[2] + part_in[4]
-    on_down.start()
-    over_y[0].wait_recv()
-    across = part_rows[1] + part_in[1] + part_in[2] + part_in[3] + part_in[4]
+    for at in (0, 4, 8):
+        spread[at].wait_recv()
+    across = part_rows[0] + part_in[8] + part_rows[1] + part_rows[2] + part_in[0] + part_in[4]
     on_up.wait_recv()
     on_down.wait_recv()
-    head_row[...] = across + part_in[5] + part_in[6]
+    head_row[...] = across + part_in[9] + part_in[10]
 
     def head_copy(target, slot):
         return send(head_row, head_in.at[row], head_send.at[slot], head_recv.at[row], {"dp": target})
@@ -406,7 +424,7 @@
         def _():
             head_copy(owner, other).wait_send()
 
-    for copy in [over_x, *over_y, on_up, on_down]:
+    for copy in [*spread, on_up, on_down]:
         copy.wait_send()
 
     @pl.when(jnp.logical_not(diagonal))
@@ -481,7 +499,7 @@
             pltpu.VMEM((seqs, tok), jnp.int32),
             pltpu.VMEM((window, STEP), jnp.float32),
             pltpu.VMEM((groups, window, STEP), jnp.bfloat16),
-            pltpu.VMEM((window, STEP), jnp.float32),
+            pltpu.VMEM((groups, window, STEP), jnp.float32),
             pltpu.VMEM((groups, window, STEP), jnp.bfloat16),
             pltpu.VMEM(wide, jnp.float32),
             pltpu.VMEM(wide, jnp.float32),
@@ -494,7 +512,7 @@
             pltpu.VMEM((HEADS, 1, width), jnp.float32),
             pltpu.VMEM((1, width), jnp.float32),
             pltpu.VMEM((3, 1, width), jnp.float32),
-            pltpu.VMEM((7, 1, width), jnp.float32),
+            pltpu.VMEM((11, 1, width), jnp.float32),
             pltpu.VMEM((1, width), jnp.float32),
             pltpu.VMEM((HEADS, 1, width), jnp.float32),
             pltpu.VMEM((8, width), jnp.float32),
@@ -507,11 +525,11 @@
             dma((HEADS,)),
             dma((HEADS,)),
             dma((1,)),
-            dma((7,)),
-            dma((7,)),
+            dma((11,)),
+            dma((11,)),
             dma((HEADS,)),
             dma((HEADS,)),
-            pltpu.SemaphoreType.REGULAR((3,)),
+            pltpu.SemaphoreType.REGULAR((4,)),
             pltpu.SemaphoreType.REGULAR((HEADS,)),
         ],
         compiler_params=pltpu.CompilerParams(

time: 58.4 us -> 58.7 us (level); the launches traced: 58.2 us -> 57.6 us
  Pallas kernels: 57.6 us -> 57 us
    pallas_call x1, Pallas kernels: 55.7 us -> 55.1 us  [on_device(): pl.pallas_call(functools.partial(body, n_ctx), out_shape=[jax.ShapeDtypeS...]
where the time goes in v3:
time: 58.7 us; the launch traced here: 57.6 us
  Pallas kernels  57 us (97%)
  between operations  0.64 us (1%)
    pallas_call x1, Pallas kernels, on_device(): pl.pallas_call(functools.partial(body, n_ctx), out_shape=[jax.ShapeDtypeS...  55.1 us
    pallas_call x1, Pallas kernels, on_device(): pl.pallas_call(deliver, out_shape=[jax.ShapeDtypeStruct(grad.shape, grad....  1.9 us

profile of v3, /device:TPU:1, one launch (start us, length us, event | category | flops | bytes accessed | tf_op | source)
XLA Modules:
  0.0 57.6 jit_solution(14401060142567653285)
XLA Ops:
  0.6 55.1 %shard_map.102 = (bf16[1024,128]{1,0:T(8,128)(2,1)}, bf16[1024,128]{1,0:T(8,128)(2,1)}, bf16[1024,128]{1,0:T(8,128)(2,1)}, f32[1,16]{1,0:T(1,128)}) custom-call(bf16[1024,128]{1,0:T(8,128)(2,1)} %bitcast.9, bf16[1024,128]{1,0:T(8,128)(2,1)} %bitcast.10, bf16[1024,128]{1,0:T(8,128)(2,1)} %bitcast.11, bf16[1024,128]{1,0:T(8,128)(2,1)} %bitcast.12, ...), custom_call_target="tpu_custom_call" | custom-call | tf_op jit(solution)/shard_map/pallas_call | solution.py:484
  55.7 1.9 %shard_map.103 = (bf16[1024,128]{1,0:T(8,128)(2,1)}, bf16[1024,128]{1,0:T(8,128)(2,1)}, bf16[1024,128]{1,0:T(8,128)(2,1)}, f32[1,16]{1,0:T(1,128)}) custom-call(bf16[1024,128]{1,0:T(8,128)(2,1)} %get-tuple-element.12.refs_0_, bf16[1024,128]{1,0:T(8,128)(2,1)} %get-tuple-element.13.refs_1_, bf16[1024,128]{1,0:T(8,128)(2,1)} %get-tuple-element.14.refs_2_, ...), custom_call_target="tpu_custom_call" | custom-call | tf_op jit(solution)/shard_map/pallas_call | solution.py:547

commit v4 on v3

--- a/solution.py
+++ b/solution.py
@@ -65,7 +65,8 @@
     def source_of(other):
         near = jnp.where(other < mine, other + 1, mine)
         late = jnp.where(other < half, mine, near)
-        early = jnp.where(other < half, mine, jnp.where(other < half + 2, half - 1, 0))
+        start = jnp.where(other > mine, other - 1, mine)
+        early = jnp.where(other < half, start, jnp.where(other < half + 2, half - 1, 0))
         return jnp.where(mine >= half, late, early)
 
     source = source_of(row)
@@ -168,8 +169,16 @@
     def _():
         for piece in (3, 2, 1, 0):
             halo_copy(0, piece, k_hbm, k_ext).start()
+
+    first_core = (d % 2 == 0) | (c == 0)
+
+    def send_values():
         for piece in (3, 2, 1, 0):
             halo_copy(1, piece, v_hbm, v_ext).start()
+
+    @pl.when((c < n_ctx - 1) & first_core)
+    def _():
+        send_values()
 
     hands_on = sum(jnp.where(feed_t, 1, 0) for feed_t in feeds) > 0
 
@@ -231,6 +240,10 @@
     def _():
         for piece in range(4):
             halo_copy(0, piece, k_hbm, k_ext).wait_recv()
+
+    @pl.when((c < n_ctx - 1) & jnp.logical_not(first_core))
+    def _():
+        send_values()
 
     pl.semaphore_signal(met.at[0], inc=1, device_id={"ctx": y_peers[2]}, device_id_type=MESH)
     pl.semaphore_signal(met.at[1], inc=1, device_id={"ctx": y_peers[3]}, device_id_type=MESH)

time: 58.7 us -> 59.4 us (1.012)
  the two profiles are of different devices: /device:TPU:1 before, /device:TPU:22 now
where the time goes in v4:
time: 59.4 us; the launch traced here: 59.2 us
  Pallas kernels  58.6 us (99%)
  between operations  0.64 us (1%)
    pallas_call x1, Pallas kernels, on_device(): pl.pallas_call(functools.partial(body, n_ctx), out_shape=[jax.ShapeDtypeS...  56.7 us
    pallas_call x1, Pallas kernels, on_device(): pl.pallas_call(deliver, out_shape=[jax.ShapeDtypeStruct(grad.shape, grad....  1.9 us

profile of v4, /device:TPU:22, one launch (start us, length us, event | category | flops | bytes accessed | tf_op | source)
XLA Modules:
  0.0 59.2 jit_solution(4501937566779314359)
XLA Ops:
  0.6 56.7 %shard_map.102 = (bf16[1024,128]{1,0:T(8,128)(2,1)}, bf16[1024,128]{1,0:T(8,128)(2,1)}, bf16[1024,128]{1,0:T(8,128)(2,1)}, f32[1,16]{1,0:T(1,128)}) custom-call(bf16[1024,128]{1,0:T(8,128)(2,1)} %bitcast.9, bf16[1024,128]{1,0:T(8,128)(2,1)} %bitcast.10, bf16[1024,128]{1,0:T(8,128)(2,1)} %bitcast.11, bf16[1024,128]{1,0:T(8,128)(2,1)} %bitcast.12, ...), custom_call_target="tpu_custom_call" | custom-call | tf_op jit(solution)/shard_map/pallas_call | solution.py:497
  57.4 1.9 %shard_map.103 = (bf16[1024,128]{1,0:T(8,128)(2,1)}, bf16[1024,128]{1,0:T(8,128)(2,1)}, bf16[1024,128]{1,0:T(8,128)(2,1)}, f32[1,16]{1,0:T(1,128)}) custom-call(bf16[1024,128]{1,0:T(8,128)(2,1)} %get-tuple-element.12.refs_0_, bf16[1024,128]{1,0:T(8,128)(2,1)} %get-tuple-element.13.refs_1_, bf16[1024,128]{1,0:T(8,128)(2,1)} %get-tuple-element.14.refs_2_, ...), custom_call_target="tpu_custom_call" | custom-call | tf_op jit(solution)/shard_map/pallas_call | solution.py:560

commit v5 on v4

--- a/solution.py
+++ b/solution.py
@@ -38,7 +38,7 @@
     dk_out, dv_out, dk_in, dv_in,
     gain_ref, gain_row, gain_in, gain_full, part_rows, part_in, head_row, head_in, part_acc,
     load_sem, halo_send, halo_recv, back_send, back_recv,
-    gain_send, gain_recv, relay_send, relay_recv, part_send, part_recv, head_send, head_recv, met, met_rows,
+    gain_send, gain_recv, relay_send, relay_recv, part_send, part_recv, head_send, head_recv, met, met_rows, here,
 ):
     tok = q_ref.shape[0]
     width = q_ref.shape[1]
@@ -197,15 +197,30 @@
     def _():
         feed(0).wait_recv()
 
+    aside = (mine == 0) & (c == 0)
+    first_of_all = aside & (row == 0)
+    hands_over = (mine == 0) & (c == 1) & (row == 1)
+    sends = [feeds[t] & jnp.logical_not(first_of_all) if t == 1 else feeds[t] for t in range(HEADS)]
+    over = send(gain_full, gain_full, relay_send.at[0], relay_recv.at[0], {"ctx": c - 1})
+
+    def tell(t):
+        pl.semaphore_signal(
+            here.at[0], inc=1, device_id={"dp": HEADS * t + mine}, device_id_type=MESH
+        )
+
     for t in range(HEADS):
 
         @pl.when(feeds[t] & (row < t))
         def _():
             pl.semaphore_wait(met_rows.at[t], 1)
 
-        @pl.when(feeds[t])
+        @pl.when(sends[t])
         def _():
             feed(t).start()
+
+    @pl.when(first_of_all)
+    def _():
+        tell(1)
 
     loads[4].wait()
     loads[5].wait()
@@ -245,28 +260,14 @@
     def _():
         send_values()
 
+    @pl.when(hands_over)
+    def _():
+        over.start()
+
     pl.semaphore_signal(met.at[0], inc=1, device_id={"ctx": y_peers[2]}, device_id_type=MESH)
     pl.semaphore_signal(met.at[1], inc=1, device_id={"ctx": y_peers[3]}, device_id_type=MESH)
     for block in range(WBLK - 1):
         k_t[:, pl.ds(block * BLK, BLK)] = k_ext[pl.ds(block * BLK, BLK)].T
-
-    def prob_grad_step(step, carry):
-        group = groups - 1 - step
-        base = pl.multiple_of(group * STEP, STEP)
-        halo_arrives(1, group, v_hbm, v_ext)
-        dp_scr[group] = dot_nt(v_ext[pl.ds(base, window)], go_ref[pl.ds(base, STEP)])
-        return carry
-
-    lax.fori_loop(0, groups, prob_grad_step, 0)
-
-    pl.semaphore_wait(met.at[0], 1)
-    pl.semaphore_wait(met.at[1], 1)
-
-    @pl.when(c < along)
-    def _():
-        pl.semaphore_wait(met.at[2], 1)
-
-    pl.semaphore_signal(met.at[3], inc=1, device_id={"ctx": far_x}, device_id_type=MESH)
 
     @pl.when(jnp.logical_not(diagonal | hands_on))
     def _():
@@ -297,11 +298,42 @@
             s_scr[chunk(kb)] = weights
             total = total + jnp.sum(weights.reshape(BLK // 8, 8, STEP), axis=0)
         inverse = 1.0 / jnp.sum(total, axis=0, keepdims=True)
+        for kb in range(kblocks):
+            p_scr[group, chunk(kb)] = (s_scr[chunk(kb)] * inverse).astype(p_scr.dtype)
+        return carry
+
+    lax.fori_loop(0, groups, query_step, 0, unroll=True)
+
+    pl.semaphore_wait(met.at[0], 1)
+    pl.semaphore_wait(met.at[1], 1)
+
+    @pl.when(c < along)
+    def _():
+        pl.semaphore_wait(met.at[2], 1)
+
+    pl.semaphore_signal(met.at[3], inc=1, device_id={"ctx": far_x}, device_id_type=MESH)
+
+    @pl.when(aside & (row >= 1) & (row < half))
+    def _():
+        pl.semaphore_wait(here.at[0], 1)
+
+    @pl.when(aside & (row >= 1) & (row < half - 1))
+    def _():
+        tell(row + 1)
+
+    @pl.when(aside & (row == half - 1))
+    def _():
+        tell(half)
+        tell(half + 1)
+
+    def grad_step(step, carry):
+        group = groups - 1 - step
+        base = pl.multiple_of(group * STEP, STEP)
+        halo_arrives(1, group, v_hbm, v_ext)
+        dp_scr[group] = dot_nt(v_ext[pl.ds(base, window)], go_ref[pl.ds(base, STEP)])
         delta = jnp.zeros((8, STEP), jnp.float32)
         for kb in range(kblocks):
-            probs = (s_scr[chunk(kb)] * inverse).astype(p_scr.dtype)
-            p_scr[group, chunk(kb)] = probs
-            products = dp_scr[group, chunk(kb)] * probs.astype(jnp.float32)
+            products = dp_scr[group, chunk(kb)] * p_scr[group, chunk(kb)].astype(jnp.float32)
             delta = delta + jnp.sum(products.reshape(BLK // 8, 8, STEP), axis=0)
         delta = jnp.sum(delta, axis=0, keepdims=True)
         for kb in range(kblocks):
@@ -318,7 +350,7 @@
         part_acc[...] += jnp.sum(products.reshape(STEP // 8, 8, width), axis=0)
         return carry
 
-    lax.fori_loop(0, groups, query_step, 0, unroll=True)
+    lax.fori_loop(0, groups, grad_step, 0, unroll=True)
 
     back_dv = send(dv_out, dv_in, back_send.at[0], back_recv.at[0], {"ctx": c - 1})
     back_dk = send(dk_out, dk_in, back_send.at[1], back_recv.at[1], {"ctx": c - 1})
@@ -387,6 +419,10 @@
     on_down.wait_recv()
     head_row[...] = across + part_in[9] + part_in[10]
 
+    @pl.when(aside & ((row == half) | (row == half + 1)))
+    def _():
+        pl.semaphore_wait(here.at[0], 1)
+
     def head_copy(target, slot):
         return send(head_row, head_in.at[row], head_send.at[slot], head_recv.at[row], {"dp": target})
 
@@ -446,9 +482,13 @@
 
     for t in range(HEADS):
 
-        @pl.when(feeds[t])
+        @pl.when(sends[t])
         def _():
             feed(t).wait_send()
+
+    @pl.when(hands_over)
+    def _():
+        over.wait_send()
 
     @pl.when(c < n_ctx - 1)
     def _():
@@ -544,6 +584,7 @@
             dma((HEADS,)),
             pltpu.SemaphoreType.REGULAR((4,)),
             pltpu.SemaphoreType.REGULAR((HEADS,)),
+            pltpu.SemaphoreType.REGULAR((1,)),
         ],
         compiler_params=pltpu.CompilerParams(
             collective_id=0, has_side_effects=True, vmem_limit_bytes=60 << 20

time: 59.4 us -> 56.1 us (0.944)
  the two profiles are of different devices: /device:TPU:22 before, /device:TPU:1 now
where the time goes in v5:
time: 56.1 us; the launch traced here: 55.6 us
  Pallas kernels  55 us (98%)
  between operations  0.64 us (1%)
    pallas_call x1, Pallas kernels, on_device(): pl.pallas_call(functools.partial(body, n_ctx), out_shape=[jax.ShapeDtypeS...  53.1 us
    pallas_call x1, Pallas kernels, on_device(): pl.pallas_call(deliver, out_shape=[jax.ShapeDtypeStruct(grad.shape, grad....  1.9 us

profile of v5, /device:TPU:1, one launch (start us, length us, event | category | flops | bytes accessed | tf_op | source)
XLA Modules:
  0.0 55.6 jit_solution(10438907041790932583)
XLA Ops:
  0.6 53.1 %shard_map.102 = (bf16[1024,128]{1,0:T(8,128)(2,1)}, bf16[1024,128]{1,0:T(8,128)(2,1)}, bf16[1024,128]{1,0:T(8,128)(2,1)}, f32[1,16]{1,0:T(1,128)}) custom-call(bf16[1024,128]{1,0:T(8,128)(2,1)} %bitcast.9, bf16[1024,128]{1,0:T(8,128)(2,1)} %bitcast.10, bf16[1024,128]{1,0:T(8,128)(2,1)} %bitcast.11, bf16[1024,128]{1,0:T(8,128)(2,1)} %bitcast.12, ...), custom_call_target="tpu_custom_call" | custom-call | tf_op jit(solution)/shard_map/pallas_call | solution.py:537
  53.7 1.9 %shard_map.103 = (bf16[1024,128]{1,0:T(8,128)(2,1)}, bf16[1024,128]{1,0:T(8,128)(2,1)}, bf16[1024,128]{1,0:T(8,128)(2,1)}, f32[1,16]{1,0:T(1,128)}) custom-call(bf16[1024,128]{1,0:T(8,128)(2,1)} %get-tuple-element.12.refs_0_, bf16[1024,128]{1,0:T(8,128)(2,1)} %get-tuple-element.13.refs_1_, bf16[1024,128]{1,0:T(8,128)(2,1)} %get-tuple-element.14.refs_2_, ...), custom_call_target="tpu_custom_call" | custom-call | tf_op jit(solution)/shard_map/pallas_call | solution.py:601

commit v6 on v5

--- a/solution.py
+++ b/solution.py
@@ -304,6 +304,36 @@
 
     lax.fori_loop(0, groups, query_step, 0, unroll=True)
 
+    back_dv = send(dv_out, dv_in, back_send.at[0], back_recv.at[0], {"ctx": c - 1})
+    back_dk = send(dk_out, dk_in, back_send.at[1], back_recv.at[1], {"ctx": c - 1})
+
+    def key_grads():
+        def step(group, carry):
+            base = pl.multiple_of(group * STEP, STEP)
+            dk_acc[pl.ds(base, window)] += jnp.dot(
+                ds_scr[group], scaled[pl.ds(base, STEP)], preferred_element_type=jnp.float32
+            )
+            return carry
+
+        lax.fori_loop(0, groups, step, 0)
+        dk_out[...] = (dk_acc[pl.ds(0, HALO)] * score_scale).astype(dk_out.dtype)
+
+    def value_grads():
+        def step(group, carry):
+            base = pl.multiple_of(group * STEP, STEP)
+            dv_acc[pl.ds(base, window)] += jnp.dot(
+                p_scr[group], go_ref[pl.ds(base, STEP)], preferred_element_type=jnp.float32
+            )
+            return carry
+
+        lax.fori_loop(0, groups, step, 0)
+        dv_out[...] = dv_acc[pl.ds(0, HALO)].astype(dv_out.dtype)
+
+        @pl.when(c > 0)
+        def _():
+            back_dv.start()
+
+    value_grads()
     pl.semaphore_wait(met.at[0], 1)
     pl.semaphore_wait(met.at[1], 1)
 
@@ -352,39 +382,6 @@
 
     lax.fori_loop(0, groups, grad_step, 0, unroll=True)
 
-    back_dv = send(dv_out, dv_in, back_send.at[0], back_recv.at[0], {"ctx": c - 1})
-    back_dk = send(dk_out, dk_in, back_send.at[1], back_recv.at[1], {"ctx": c - 1})
-
-    def key_grads():
-        def step(group, carry):
-            base = pl.multiple_of(group * STEP, STEP)
-            dk_acc[pl.ds(base, window)] += jnp.dot(
-                ds_scr[group], scaled[pl.ds(base, STEP)], preferred_element_type=jnp.float32
-            )
-            return carry
-
-        lax.fori_loop(0, groups, step, 0)
-        dk_out[...] = (dk_acc[pl.ds(0, HALO)] * score_scale).astype(dk_out.dtype)
-
-        @pl.when(c > 0)
-        def _():
-            back_dk.start()
-
-    def value_grads():
-        def step(group, carry):
-            base = pl.multiple_of(group * STEP, STEP)
-            dv_acc[pl.ds(base, window)] += jnp.dot(
-                p_scr[group], go_ref[pl.ds(base, STEP)], preferred_element_type=jnp.float32
-            )
-            return carry
-
-        lax.fori_loop(0, groups, step, 0)
-        dv_out[...] = dv_acc[pl.ds(0, HALO)].astype(dv_out.dtype)
-
-        @pl.when(c > 0)
-        def _():
-            back_dv.start()
-
     part_rows[0] = jnp.sum(part_acc[...], axis=0, keepdims=True)
 
     def part_copy(source, slot, target):
@@ -398,7 +395,6 @@
     pl.semaphore_wait(met.at[3], 1)
     for copy in spread:
         copy.start()
-    value_grads()
     key_grads()
     spread[2].wait_recv()
     spread[6].wait_recv()
@@ -436,6 +432,10 @@
         @pl.when(owner == d)
         def _():
             head_in[row] = head_row[...]
+
+    @pl.when(c > 0)
+    def _():
+        back_dk.start()
 
     @pl.when(c < n_ctx - 1)
     def _():

time: 56.1 us -> 57.2 us (1.020)
  the two profiles are of different devices: /device:TPU:1 before, /device:TPU:62 now
where the time goes in v6:
time: 57.2 us; the launch traced here: 57 us
  Pallas kernels  56.4 us (99%)
  between operations  0.64 us (1%)
    pallas_call x1, Pallas kernels, on_device(): pl.pallas_call(functools.partial(body, n_ctx), out_shape=[jax.ShapeDtypeS...  54.5 us
    pallas_call x1, Pallas kernels, on_device(): pl.pallas_call(deliver, out_shape=[jax.ShapeDtypeStruct(grad.shape, grad....  1.9 us

profile of v6, /device:TPU:62, one launch (start us, length us, event | category | flops | bytes accessed | tf_op | source)
XLA Modules:
  0.0 57.0 jit_solution(4116995855691308327)
XLA Ops:
  0.6 54.5 %shard_map.102 = (bf16[1024,128]{1,0:T(8,128)(2,1)}, bf16[1024,128]{1,0:T(8,128)(2,1)}, bf16[1024,128]{1,0:T(8,128)(2,1)}, f32[1,16]{1,0:T(1,128)}) custom-call(bf16[1024,128]{1,0:T(8,128)(2,1)} %bitcast.9, bf16[1024,128]{1,0:T(8,128)(2,1)} %bitcast.10, bf16[1024,128]{1,0:T(8,128)(2,1)} %bitcast.11, bf16[1024,128]{1,0:T(8,128)(2,1)} %bitcast.12, ...), custom_call_target="tpu_custom_call" | custom-call | tf_op jit(solution)/shard_map/pallas_call | solution.py:537
  55.1 1.9 %shard_map.103 = (bf16[1024,128]{1,0:T(8,128)(2,1)}, bf16[1024,128]{1,0:T(8,128)(2,1)}, bf16[1024,128]{1,0:T(8,128)(2,1)}, f32[1,16]{1,0:T(1,128)}) custom-call(bf16[1024,128]{1,0:T(8,128)(2,1)} %get-tuple-element.12.refs_0_, bf16[1024,128]{1,0:T(8,128)(2,1)} %get-tuple-element.13.refs_1_, bf16[1024,128]{1,0:T(8,128)(2,1)} %get-tuple-element.14.refs_2_, ...), custom_call_target="tpu_custom_call" | custom-call | tf_op jit(solution)/shard_map/pallas_call | solution.py:601
